TPU v7x, 256 devices: a whole 4x4x8 slice. The times are simulated.
256 devices in a mesh: bead: 64 (over x, z, y_hi), slab: 4 (over y_lo, core).
Axes of the slice: x: 4, y: 4 (y_hi: 2, y_lo: 2; y = y_hi * 2 + y_lo), z: 8, core: 2. Of those that a mesh axis runs over, the one named last changes fastest.
Arguments:
- section: float32 [64, 3, 16384], P('bead', None, 'slab'), may hold values from -0.4 to 12, as said below
- momentum: float32 [64, 3, 16384], P('bead', None, 'slab'), may hold values from -6 to 6
- neighbours: int32 [4, 32, 8], P('slab'), may hold values from 0 to 39
- border_rows: int32 [4, 2, 512], P('slab'), may hold values from 0 to 2047
- counts: int32 [4], P('slab'), may hold values from 2048 to 4096
Outputs:
- new_section: float32 [64, 3, 16384], P('bead', None, 'slab')
- new_momentum: float32 [64, 3, 16384], P('bead', None, 'slab')
Inputs may be any that keep to these rules, and one draw needn't show every extreme that they name: section[0] holds positions whose component 0 lies in its slab's range [3 s, 3 s + 3) and components 1 and 2 in [0, 3); the other beads hold displacements within 0.4. `border_rows`: every listed halo row is below the sending slab's count.
All inputs are finite; a program needn't handle non-finite values.
Results may differ from a plain program's by a relative error of at most 0.0003.
Values sent between devices are 32-bit elements; how exact they have to be, the bound alone decides.
A program may use at most 64 MiB of HBM per device.

v0:
```python
import math

import jax
import jax.numpy as jnp
from jax import lax
from jax.sharding import PartitionSpec as P

time_step = 0.1
omega_sq = 4.0
slab_width = 3.0
cut_sq = 16.0


def broadcast(value, axis, root):
    mine = lax.axis_index(axis) == root
    return lax.psum(jnp.where(mine, value, jnp.zeros_like(value)), axis)


def prefix(value, axis, combine, identity):
    size, index = (lax.axis_size(axis), lax.axis_index(axis))
    everything = lax.all_gather(value, axis)
    start = jnp.broadcast_to(jnp.asarray(identity, value.dtype), value.shape)

    def step(k, before):
        at = size - 1 - k
        reached = at > index
        new = combine(before, everything[at])
        return jnp.where(reached, new, before)

    return lax.fori_loop(0, size, step, start)


def shifted(value, axis, steps):
    count = lax.axis_size(axis)
    pairs = [(source, (source + steps) % count) for source in range(count)]
    return lax.ppermute(value, axis, pairs)


def pair_forces(atom_places, lower, upper, neighbours, count):
    tile = 128
    layer_width = atom_places.shape[1]
    halo = lower.shape[1]
    extended = jnp.concatenate([lower, atom_places, upper], axis=1)
    rows = jnp.arange(extended.shape[1], dtype=jnp.int32)
    live = jnp.logical_or(rows < halo, rows >= halo + layer_width)
    live = jnp.logical_or(live, rows - halo < count)
    ext_mask = live.astype(jnp.float32).reshape(-1, tile)
    ext_tiles = extended.reshape(3, -1, tile)
    tiles = layer_width // tile
    group = math.gcd(tiles, 8)
    own = atom_places.reshape(3, tiles // group, group, tile).transpose(1, 0, 2, 3)
    lists = neighbours.reshape(tiles // group, group, -1)

    def block(item):
        own_block, list_block = item
        partner = ext_tiles[:, list_block].reshape(3, group, -1)
        weight = ext_mask[list_block].reshape(group, -1)
        diff = own_block[:, :, :, None] - partner[:, :, None, :]
        dist = jnp.sum(diff * diff, axis=0)
        inverse = 1.0 / (dist + 1.0)
        inv_two = inverse * inverse
        inv_four = inv_two * inv_two
        inv_seven = inv_four * inv_two * inverse
        cutoff = jnp.maximum(1.0 - dist / cut_sq, 0.0)
        factor = (48.0 * inv_seven - 24.0 * inv_four) * cutoff * cutoff * weight[:, None, :]
        return jnp.sum(diff * factor[None], axis=-1)

    result = lax.map(block, (own, lists))
    force = result.transpose(1, 0, 2, 3).reshape(3, layer_width)
    own_live = (jnp.arange(layer_width, dtype=jnp.int32) < count).astype(jnp.float32)
    return force * own_live[None, :]


def adding(earlier, later):
    return earlier + later


def body(section, momentum, neighbours, border_rows, counts):
    bead_replicas = lax.axis_size("bead")
    level = lax.axis_index("bead").astype(jnp.float32)
    safe_level = jnp.maximum(level, 1.0)
    coords = section[0]
    first = broadcast(coords, "bead", 0)
    scaled = jnp.where(level > 0, coords / safe_level, 0.0)
    suffix = prefix(scaled, "bead", adding, jnp.zeros_like(scaled))
    atom_places = jnp.where(level > 0, first + level * (suffix + scaled), coords)
    slab_layers = lax.axis_size("slab")
    slab_id = lax.axis_index("slab")
    box = slab_width * slab_layers
    first_axis = jnp.array([1.0, 0.0, 0.0], dtype=jnp.float32)[:, None]
    upward_send = atom_places[:, border_rows[0, 0]]
    downward_send = atom_places[:, border_rows[0, 1]]
    lower = shifted(upward_send, "slab", 1)
    upper = shifted(downward_send, "slab", -1)
    lower = lower - jnp.where(slab_id == 0, box, 0.0) * first_axis
    upper = upper + jnp.where(slab_id == slab_layers - 1, box, 0.0) * first_axis
    bead_force = pair_forces(atom_places, lower, upper, neighbours[0], counts[0]) / float(
        bead_replicas
    )
    weighted = level * bead_force
    after = prefix(weighted, "bead", adding, jnp.zeros_like(weighted))
    total, weighted_total = lax.psum((bead_force, weighted), "bead")
    section_force = jnp.where(level > 0, (weighted_total - after) / safe_level, total)
    mass = jnp.where(level > 0, (level + 1.0) / safe_level, 1.0)
    spring = jnp.where(level > 0, omega_sq * mass, 0.0)
    step = time_step / 3.0
    p = momentum[0] + 0.5 * time_step * section_force
    u = coords
    for turn in range(3):
        p = p - 0.5 * step * spring * u
        u = u + step * p / mass
        p = p - 0.5 * step * spring * u
    return (u[None], p[None])


def solution(mesh):
    return jax.shard_map(
        body,
        mesh=mesh,
        in_specs=(
            P("bead", None, "slab"),
            P("bead", None, "slab"),
            P("slab", None, None),
            P("slab", None, None),
            P("slab"),
        ),
        out_specs=(P("bead", None, "slab"), P("bead", None, "slab")),
        check_vma=False,
    )
```

profile of v0, /device:TPU:2, one launch (start us, length us, event | category | flops | bytes accessed | tf_op | source)
XLA Modules:
  0.0 1240.5 jit_solution(6940184823683874336)
XLA Ops:
  7.2 1.5 fusion.20
  11.1 332.9 %psum.21 = f32[3,4096]{1,0:T(4,128)S(1)} all-reduce(f32[3,4096]{1,0:T(4,128)S(1)} %fusion.17), channel_id=1, replica_groups=mesh['bead'=64,'slab'=4] {'bead'}, use_global_device_ids=true, to_apply=%region_0.1 | all-reduce | flops 12288 | bytes 98304 | tf_op jit(solution)/shard_map/psum | solution.py:16
  345.5 59.7 %while.44 = (s32[]{:T(128)}, f32[3,4096]{1,0:T(4,128)S(1)}, s32[]{:T(128)}, f32[64,3,4096]{2,1,0:T(4,128)}, s32[]{:T(128)}, /*index=5*/s32[]{:T(128)}, s32[]{:T(128)}, s32[]{:T(128)}) while((s32[]{:T(128)}, f32[3,4096]{1,0:T(4,128)S(1)}, s32[]{:T(128)}, f32[64,3,4096]{2,1,0:T(4,128)}, s32[]{:T(128)}, /*index=5*/s32[]{:T(128)}, ...), condition=%wide.region_2.3_spmd.clone, body=%wide.region_1.2_spmd.clone.sunk | while | flops 36872 | bytes 147611 | solution.py:30
  347.3 0.9 add_select_fusion.4
  352.0 0.9 add_select_fusion.4
  365.1 0.9 add_select_fusion.4
  369.7 0.9 add_select_fusion.4
  382.8 0.9 add_select_fusion.4
  406.7 1.0 gather_fusion.3
  407.9 1.0 gather_fusion.2
  409.7 2.5 collective-permute-done
  412.3 42.8 %while.43 = (s32[]{:T(128)}, f32[4,3,8,128]{3,2,1,0:T(8,128)S(1)}, f32[4,3,8,128]{3,2,1,0:T(8,128)S(1)}, s32[4,8,8]{2,1,0:T(8,128)S(1)}, f32[3,40,128]{2,0,1:T(4,128)S(1)}, /*index=5*/s32[]{:T(128)}, s32[]{:T(128)}) while((s32[]{:T(128)}, f32[4,3,8,128]{3,2,1,0:T(8,128)S(1)}, f32[4,3,8,128]{3,2,1,0:T(8,128)S(1)}, ...), condition=%wide.region_6.7_spmd.clone, body=%wide.region_3.6_spmd.clone.sunk | while | flops 33598656 | bytes 17839964 | solution.py:68
  413.2 3.2 fusion.32
  417.6 3.7 fusion.34
  421.3 1.7 fusion.35
  423.9 3.2 fusion.32
  428.3 3.7 fusion.34
  432.0 1.7 fusion.35
  434.6 3.2 fusion.32
  439.0 3.7 fusion.34
  442.7 1.7 fusion.35
  445.3 3.2 fusion.32
  449.8 3.7 fusion.34
  453.4 1.7 fusion.35
  456.7 146.9 %all-gather.5.cloned.1.call-done = f32[64,3,4096]{2,1,0:T(4,128)} async-done(((f32[1,3,4096]{2,1,0:T(4,128)}), f32[64,3,4096]{2,1,0:T(4,128)}) %all-gather.5.cloned.1.call-update) | async-done | bytes 3145744 | tf_op jit(solution)/shard_map/all_gather | solution.py:21
  603.6 59.7 %while.45 = (s32[]{:T(128)}, f32[3,4096]{1,0:T(4,128)S(1)}, s32[]{:T(128)}, f32[64,3,4096]{2,1,0:T(4,128)}, s32[]{:T(128)}, /*index=5*/s32[]{:T(128)}, s32[]{:T(128)}, s32[]{:T(128)}) while((s32[]{:T(128)}, f32[3,4096]{1,0:T(4,128)S(1)}, s32[]{:T(128)}, f32[64,3,4096]{2,1,0:T(4,128)}, s32[]{:T(128)}, /*index=5*/s32[]{:T(128)}, ...), condition=%wide.region_9.10_spmd.clone, body=%wide.region_8.9_spmd.clone.sunk | while | flops 36872 | bytes 147611 | solution.py:30
  613.9 0.9 add_select_fusion.5
  621.3 0.9 add_select_fusion.5
  622.3 0.9 add_select_fusion.5
  624.1 0.9 add_select_fusion.5
  625.1 0.9 add_select_fusion.5
  631.6 0.9 add_select_fusion.5
  632.5 0.9 add_select_fusion.5
  633.5 0.9 add_select_fusion.5
  634.4 0.9 add_select_fusion.5
  640.9 0.9 add_select_fusion.5
  641.9 0.9 add_select_fusion.5
  643.7 0.9 add_select_fusion.5
  644.7 0.9 add_select_fusion.5
  651.2 0.9 add_select_fusion.5
  652.1 0.9 add_select_fusion.5
  653.1 0.9 add_select_fusion.5
  654.0 0.9 add_select_fusion.5
  655.0 0.9 add_select_fusion.5
  661.5 0.9 add_select_fusion.5
  662.4 0.9 add_select_fusion.5
  663.3 568.3 %all-reduce.3.cloned.1.call-done = (f32[3,4096]{1,0:T(4,128)}, f32[3,4096]{1,0:T(4,128)}) async-done(((f32[3,4096]{1,0:T(4,128)}, f32[3,4096]{1,0:T(4,128)}), (f32[3,4096]{1,0:T(4,128)}, f32[3,4096]{1,0:T(4,128)})) %all-reduce.3.cloned.1.call-update) | async-done | bytes 98320 | tf_op jit(solution)/shard_map/psum | solution.py:102
  1231.6 1.0 subtract_bitcast_fusion
  (186 shorter events, 111.2 us)
Async XLA Ops:
  7.2 338.3 %all-gather.3.cloned.1.call-start = ((), (), s32[]{:S(2)}) async-start(), calls=%async_computation | async-start | bytes 4259840 | tf_op jit(solution)/shard_map/all_gather | solution.py:21
  8.7 594.9 %all-gather.5.cloned.1.call-start = ((), (), s32[]{:S(2)}) async-start(), calls=%async_computation.1 | async-start | bytes 4259840 | tf_op jit(solution)/shard_map/all_gather | solution.py:21
  407.8 1.8 collective-permute-start.1
  409.1 3.1 collective-permute-start
  412.3 819.3 %copy-start = (f32[1,3,4096]{2,0,1:T(1,128)S(1)}, f32[1,3,4096]{2,0,1:T(1,128)}, u32[]{:S(2)}) copy-start(f32[1,3,4096]{2,0,1:T(1,128)} %param.12) | copy-start | bytes 147460
  412.3 819.3 %copy-start.1 = (f32[1,3,4096]{2,0,1:T(1,128)S(1)}, f32[1,3,4096]{2,0,1:T(1,128)}, u32[]{:S(2)}) copy-start(f32[1,3,4096]{2,0,1:T(1,128)} %param.13) | copy-start | bytes 147460
  455.9 775.7 %all-reduce.3.cloned.1.call-start = ((), (), s32[]{:S(2)}) async-start(), calls=%async_computation.2 | async-start | bytes 262144 | tf_op jit(solution)/shard_map/psum | solution.py:102
Sparse Core Ops, SparseCore 0:
  11.5 131.0 all-gather.2
  456.0 147.5 all-gather.4
  606.3 625.2 all-reduce.2
where the time goes:
time: 1250 us; the launch traced here: 1240 us
  waiting for transfers between devices  718 us (57%)
  blocking collectives  333 us (27%)
  other arithmetic  161 us (13%)
  between operations  14.6 us (1%)
    psum x1, waiting for transfers between devices, body(): total, weighted_total = lax.psum((bead_force, weighted), 'bead')  568 us
    psum x1, blocking collectives, broadcast(): return lax.psum(jnp.where(mine, value, jnp.zeros_like(value)), axis)  333 us
    all_gather x2, waiting for transfers between devices, prefix(): everything = lax.all_gather(value, axis)  147 us
    select_n x128, other arithmetic, step(): return jnp.where(reached, new, before)  117 us
  transfers between devices with their start and end apart: 5, of which 3 were waited for; matrix products, arithmetic and copies ran while one was open for 5% of the time, Pallas kernels for 0%

commit v1 on v0

v1 whole, which is shorter than its diff:
```python
import functools

import jax
import jax.numpy as jnp
from jax import lax
from jax.experimental import pallas as pl
from jax.experimental.pallas import tpu as pltpu
from jax.sharding import PartitionSpec as P

MESH = pl.DeviceIdType.MESH
time_step = 0.1
omega_sq = 4.0
slab_width = 3.0
NX, NZ, NY = 4, 8, 2
TILE = 128
KROWS = 32
F32 = jnp.float32
BF16 = jnp.bfloat16


def place():
    bead = lax.axis_index("bead")
    x = bead // (NZ * NY)
    z = (bead // NY) % NZ
    y = bead % NY
    return x, z, y


def bead_of(x, z, y):
    return (x * NZ + z) * NY + y


def to_bead(bead):
    return (bead, lax.axis_index("slab"))


def group_steps():
    return [(dz, dy) for dz in range(NZ) for dy in range(NY) if dz or dy]


def greet(extra=()):
    x, z, y = place()
    barrier = pltpu.get_barrier_semaphore()
    count = 0
    for dz, dy in group_steps():
        target = bead_of(x, (z + dz) % NZ, (y + dy) % NY)
        pl.semaphore_signal(barrier, inc=1, device_id=to_bead(target), device_id_type=MESH)
        count += 1
    for dx in range(1, NX):
        target = bead_of((x + dx) % NX, z, y)
        pl.semaphore_signal(barrier, inc=1, device_id=to_bead(target), device_id_type=MESH)
        count += 1
    for device in extra:
        pl.semaphore_signal(barrier, inc=1, device_id=device, device_id_type=MESH)
        count += 1
    pl.semaphore_wait(barrier, count)


def slot_of(dz, dy):
    return dz * NY + dy


def scatter_chunks(src, r1, send_sem, recv_sem, width):
    x, z, y = place()
    copies = []
    for k, (dz, dy) in enumerate(group_steps()):
        tz = (z + dz) % NZ
        copy = pltpu.make_async_remote_copy(
            src_ref=src.at[:, pl.ds(pl.multiple_of(tz * width, width), width)],
            dst_ref=r1.at[slot_of(dz, dy)],
            send_sem=send_sem.at[k],
            recv_sem=recv_sem.at[k],
            device_id=to_bead(bead_of(x, tz, (y + dy) % NY)),
            device_id_type=MESH,
        )
        copy.start()
        copies.append(copy)
    return copies


def exchange_x(t2, r2, send_sem, recv_sem):
    x, z, y = place()
    copies = []
    for dx in range(1, NX):
        copy = pltpu.make_async_remote_copy(
            src_ref=t2,
            dst_ref=r2.at[dx],
            send_sem=send_sem.at[dx],
            recv_sem=recv_sem.at[dx],
            device_id=to_bead(bead_of((x + dx) % NX, z, y)),
            device_id_type=MESH,
        )
        copy.start()
        copies.append(copy)
    return copies


def return_chunk(px, full, tz, dz, send_sem, recv_sem, width):
    x, z, y = place()
    copy = pltpu.make_async_remote_copy(
        src_ref=px.at[tz],
        dst_ref=full.at[:, pl.ds(pl.multiple_of(z * width, width), width)],
        send_sem=send_sem.at[dz],
        recv_sem=recv_sem.at[dz],
        device_id=to_bead(bead_of(x, tz, y)),
        device_id_type=MESH,
    )
    copy.start()
    return copy


def level_rows(bead, shape):
    return jnp.full(shape, bead.astype(F32), F32)


def forward_scan(section, r1, t2, r2, px, full, sems):
    s1, q1, s2, q2, s3, q3 = sems
    x, z, y = place()
    width = section.shape[1] // NZ
    shape = (3, width)
    sent = scatter_chunks(section, r1, s1, q1, width)
    r1[0] = section[:, pl.ds(pl.multiple_of(z * width, width), width)]
    for copy in sent:
        copy.wait_recv()

    def source(zs, ys):
        slot = ((z + (NZ - zs)) % NZ) * NY + (y + (NY - ys)) % NY
        return r1[slot]

    total = jnp.zeros(shape, F32)
    for zs in reversed(range(NZ)):
        kept = None
        for ys in reversed(range(NY)):
            level = level_rows(bead_of(x, zs, ys), (1, width))
            inverse = jnp.where(level > 0, 1.0 / jnp.maximum(level, 1.0), 0.0)
            total = total + source(zs, ys) * inverse
            kept = total if kept is None else jnp.where(y == ys, total, kept)
        px[zs] = kept
    t2[0] = total
    t2[1] = source(0, 0)
    swapped = exchange_x(t2, r2, s2, q2)
    for copy in swapped:
        copy.wait_recv()
    base = jnp.zeros(shape, F32)
    first = source(0, 0)
    for dx in range(1, NX):
        xs = (x + (NX - dx)) % NX
        base = base + jnp.where(xs > x, r2[dx, 0], 0.0)
        first = jnp.where(xs == 0, r2[dx, 1], first)
    returned = []
    for dz in list(range(1, NZ)) + [0]:
        tz = (z + dz) % NZ
        level = level_rows(bead_of(x, tz, y), (1, width))
        places = first + level * (px[tz] + base)
        if dz:
            px[tz] = places
            returned.append(return_chunk(px, full, tz, dz, s3, q3, width))
        else:
            full[:, pl.ds(pl.multiple_of(z * width, width), width)] = places
    for copy in returned:
        copy.wait_recv()
    for copy in sent + swapped + returned:
        copy.wait_send()


def backward_scan(force, r1, t2, r2, px, full, sems):
    s1, q1, s2, q2, s3, q3 = sems
    x, z, y = place()
    width = force.shape[1] // NZ
    shape = (3, width)
    sent = scatter_chunks(force, r1, s1, q1, width)
    r1[0] = force[:, pl.ds(pl.multiple_of(z * width, width), width)]
    for copy in sent:
        copy.wait_recv()

    def source(zs, ys):
        slot = ((z + (NZ - zs)) % NZ) * NY + (y + (NY - ys)) % NY
        return r1[slot]

    total = jnp.zeros(shape, F32)
    plain = jnp.zeros(shape, F32)
    for zs in range(NZ):
        kept = None
        for ys in range(NY):
            level = level_rows(bead_of(x, zs, ys), (1, width))
            one = source(zs, ys)
            plain = plain + one
            total = total + one * level
            kept = total if kept is None else jnp.where(y == ys, total, kept)
        px[zs] = kept
    t2[0] = total
    t2[1] = plain
    swapped = exchange_x(t2, r2, s2, q2)
    for copy in swapped:
        copy.wait_recv()
    base = jnp.zeros(shape, F32)
    for dx in range(1, NX):
        xs = (x + (NX - dx)) % NX
        base = base + jnp.where(xs < x, r2[dx, 0], 0.0)
        plain = plain + r2[dx, 1]
    returned = []
    for dz in list(range(1, NZ)) + [0]:
        tz = (z + dz) % NZ
        level = level_rows(bead_of(x, tz, y), (1, width))
        inverse = 1.0 / jnp.maximum(level, 1.0)
        result = jnp.where(level > 0, (px[tz] + base) * inverse, plain)
        if dz:
            px[tz] = result
            returned.append(return_chunk(px, full, tz, dz, s3, q3, width))
        else:
            full[:, pl.ds(pl.multiple_of(z * width, width), width)] = result
    for copy in returned:
        copy.wait_recv()
    for copy in sent + swapped + returned:
        copy.wait_send()


def gather_rows(full, border, which, reach):
    halo = border.shape[1]
    parts = []
    for n in range(halo // TILE):
        index = jnp.broadcast_to(border[pl.ds(which, 1), pl.ds(n * TILE, TILE)], (8, TILE))
        lane, block = index % TILE, index // TILE
        out = jnp.zeros((8, TILE), F32)
        for m in range(reach // TILE):
            piece = full[:, pl.ds(m * TILE, TILE)]
            piece = jnp.concatenate([piece, jnp.zeros((5, TILE), F32)], axis=0)
            taken = jnp.take_along_axis(piece, lane, axis=1, mode="promise_in_bounds")
            out = jnp.where(block == m, taken, out)
        parts.append(out[0:3])
    return jnp.concatenate(parts, axis=1)


def slab_peers():
    slab, count = lax.axis_index("slab"), lax.axis_size("slab")
    bead = lax.axis_index("bead")
    return (bead, (slab + 1) % count), (bead, (slab + count - 1) % count)


def halo_exchange(full, border, out, edge, landed, send_sem, recv_sem):
    up_peer, down_peer = slab_peers()
    edge[0] = gather_rows(full, border, 0, full.shape[1] // 2)
    edge[1] = gather_rows(full, border, 1, full.shape[1] // 2)
    copies = []
    for k, peer in enumerate((up_peer, down_peer)):
        copy = pltpu.make_async_remote_copy(
            src_ref=edge.at[k],
            dst_ref=landed.at[k],
            send_sem=send_sem.at[k],
            recv_sem=recv_sem.at[k],
            device_id=peer,
            device_id_type=MESH,
        )
        copy.start()
        copies.append(copy)
    return copies


def forward_kernel(section, border, out, r1, t2, r2, px, full, edge, landed, *sems):
    slab, count = lax.axis_index("slab"), lax.axis_size("slab")
    greet(slab_peers())
    forward_scan(section.at[0], r1, t2, r2, px, full, sems[:6])
    copies = halo_exchange(full, border.at[0], out, edge, landed, *sems[6:])
    halo = edge.shape[2]
    rows = full.shape[1]
    out[:, pl.ds(halo, rows)] = full[...]
    for copy in copies:
        copy.wait_recv()
    box = slab_width * count
    axis = lax.broadcasted_iota(jnp.int32, (3, halo), 0)
    low = jnp.where(slab == 0, -box, 0.0)
    high = jnp.where(slab == count - 1, box, 0.0)
    out[:, pl.ds(0, halo)] = landed[0] + jnp.where(axis == 0, low, 0.0)
    out[:, pl.ds(halo + rows, halo)] = landed[1] + jnp.where(axis == 0, high, 0.0)
    for copy in copies:
        copy.wait_send()


def backward_kernel(force, section, momentum, new_section, new_momentum, r1, t2, r2, px, full, *sems):
    greet()
    backward_scan(force, r1, t2, r2, px, full, sems[:6])
    bead = lax.axis_index("bead")
    shape = (1, full.shape[1])
    level = level_rows(bead, shape)
    safe = jnp.maximum(level, 1.0)
    mass = jnp.where(level > 0, (level + 1.0) / safe, 1.0)
    spring = jnp.where(level > 0, omega_sq * mass, 0.0)
    step = time_step / 3.0
    p = momentum[0] + (0.5 * time_step) * full[...]
    u = section[0]
    push = 0.5 * step * spring
    drift = step / mass
    for turn in range(3):
        p = p - push * u
        u = u + drift * p
        p = p - push * u
    new_section[0] = u
    new_momentum[0] = p


def split3(value):
    high = value.astype(BF16).astype(F32)
    rest = value - high
    middle = rest.astype(BF16).astype(F32)
    low = rest - middle
    return high, middle, low


def prepare_tile(places, centre, live):
    p = places - centre
    norm = jnp.sum(p * p, axis=0, keepdims=True)
    high, middle, low = split3(p)
    far = jnp.where(live, norm, 4096.0)
    ones = jnp.ones((3, TILE), F32)
    pad = jnp.zeros((KROWS - 24, TILE), F32)
    left = jnp.concatenate([high, high, middle, middle, high, low, *split3(far), ones, pad], axis=0)
    h2, m2, l2 = -2.0 * high, -2.0 * middle, -2.0 * low
    right = jnp.concatenate([h2, m2, h2, m2, l2, h2, ones, *split3(norm + 1.0), pad], axis=0)
    return left, right


def force_kernel(counts, neighbours, ext, out, lefts, lefts_t, rights):
    slab = lax.axis_index("slab")
    rows = out.shape[1]
    tiles = rows // TILE
    ext_tiles = ext.shape[1] // TILE
    halo_tiles = (ext_tiles - tiles) // 2
    count = counts[0]
    axis = lax.broadcasted_iota(jnp.int32, (3, TILE), 0)
    middle = (slab.astype(F32) + 0.5) * slab_width
    centre = jnp.where(axis == 0, middle, 0.5 * slab_width)
    lane = lax.broadcasted_iota(jnp.int32, (1, TILE), 1)

    def prepare(t, carry):
        places = ext[:, pl.ds(pl.multiple_of(t * TILE, TILE), TILE)]
        row = (t - halo_tiles) * TILE + lane
        live = (row < 0) | (row >= rows) | (row < count)
        left, right = prepare_tile(places, centre, live)
        lefts[t] = left.astype(BF16)
        lefts_t[t] = left.T.astype(BF16)
        rights[t] = right.astype(BF16)
        return carry

    lax.fori_loop(0, ext_tiles, prepare, 0)
    listed = neighbours.shape[2]

    def tile_force(i, carry):
        right = rights[i + halo_tiles]
        total = jnp.zeros((KROWS, TILE), F32)
        for n in range(0, listed, 2):
            pair = [neighbours[0, i, n], neighbours[0, i, n + 1]]
            factors = []
            for t in pair:
                q = jnp.dot(lefts_t[t], right, preferred_element_type=F32)
                r = 1.0 / q
                r2 = r * r
                c = jnp.maximum(17.0 - q, 0.0) * r2
                factors.append(((c * c) * (r2 * r - 0.5)).astype(BF16))
            f = jnp.concatenate(factors, axis=0)
            x = jnp.concatenate([lefts[t] for t in pair], axis=1)
            total = total + jnp.dot(x, f, preferred_element_type=F32)
        first = pl.multiple_of(i * TILE, TILE)
        mine = ext[:, pl.ds(pl.multiple_of(first + halo_tiles * TILE, TILE), TILE)] - centre
        moved = total[0:3] + total[6:9] + total[15:18]
        scale = jnp.where(first + lane < count, 48.0 / 256.0 / lax.axis_size("bead"), 0.0)
        out[:, pl.ds(first, TILE)] = (mine * total[21:22] - moved) * scale
        return carry

    lax.fori_loop(0, tiles, tile_force, 0)


def scan_scratch(rows):
    width = rows // NZ
    dma = pltpu.SemaphoreType.DMA
    return [
        pltpu.VMEM((NZ * NY, 3, width), F32),
        pltpu.VMEM((2, 3, width), F32),
        pltpu.VMEM((NX, 2, 3, width), F32),
        pltpu.VMEM((NZ, 3, width), F32),
        pltpu.VMEM((3, rows), F32),
    ], [
        dma((NZ * NY,)), dma((NZ * NY,)), dma((NX,)), dma((NX,)), dma((NZ,)), dma((NZ,)),
    ]


VM = pl.BlockSpec(memory_space=pltpu.VMEM)
SM = pl.BlockSpec(memory_space=pltpu.SMEM)


def forward(section, border_rows):
    rows, halo = section.shape[2], border_rows.shape[2]
    buffers, sems = scan_scratch(rows)
    dma = pltpu.SemaphoreType.DMA
    return pl.pallas_call(
        forward_kernel,
        out_shape=jax.ShapeDtypeStruct((3, rows + 2 * halo), F32),
        in_specs=[VM, VM],
        out_specs=VM,
        scratch_shapes=buffers
        + [pltpu.VMEM((2, 3, halo), F32)] * 2
        + sems
        + [dma((2,)), dma((2,))],
        compiler_params=pltpu.CompilerParams(collective_id=0, has_side_effects=True),
        name="forward_scan",
    )(section, border_rows)


def forces(ext, neighbours, counts, rows):
    ext_tiles = ext.shape[1] // TILE
    return pl.pallas_call(
        force_kernel,
        out_shape=jax.ShapeDtypeStruct((3, rows), F32),
        in_specs=[SM, SM, VM],
        out_specs=VM,
        scratch_shapes=[
            pltpu.VMEM((ext_tiles, KROWS, TILE), BF16),
            pltpu.VMEM((ext_tiles, TILE, KROWS), BF16),
            pltpu.VMEM((ext_tiles, KROWS, TILE), BF16),
        ],
        name="pair_forces",
    )(counts, neighbours, ext)


def backward(force, section, momentum):
    rows = section.shape[2]
    buffers, sems = scan_scratch(rows)
    like = jax.ShapeDtypeStruct(section.shape, F32)
    return pl.pallas_call(
        backward_kernel,
        out_shape=(like, like),
        in_specs=[VM, VM, VM],
        out_specs=(VM, VM),
        scratch_shapes=buffers + sems,
        compiler_params=pltpu.CompilerParams(collective_id=1, has_side_effects=True),
        name="backward_scan",
    )(force, section, momentum)


def body(section, momentum, neighbours, border_rows, counts):
    ext = forward(section, border_rows)
    force = forces(ext, neighbours, counts, section.shape[2])
    return backward(force, section, momentum)


def solution(mesh):
    return jax.shard_map(
        body,
        mesh=mesh,
        in_specs=(
            P("bead", None, "slab"),
            P("bead", None, "slab"),
            P("slab", None, None),
            P("slab", None, None),
            P("slab"),
        ),
        out_specs=(P("bead", None, "slab"), P("bead", None, "slab")),
        check_vma=False,
    )
```

time: 1250 us -> 86.2 us (0.07)
  waiting for transfers between devices: 718 us -> 0 us
  blocking collectives: 333 us -> 0 us
  other arithmetic: 161 us -> 0 us
  Pallas kernels: 0 us -> 77.4 us
  between operations: 14.6 us -> 1.3 us
    psum x1 -> x0, waiting for transfers between devices: 568 us -> none  [body(): total, weighted_total = lax.psum((bead_force, weighted), 'bead')]
    psum x1 -> x0, blocking collectives: 333 us -> none  [broadcast(): return lax.psum(jnp.where(mine, value, jnp.zeros_like(value)), axis)]
    all_gather x2 -> x0, waiting for transfers between devices: 147 us -> none  [prefix(): everything = lax.all_gather(value, axis)]
    select_n x136 -> x0, other arithmetic: 121 us -> none  [the longest x128 117 us: step(): return jnp.where(reached, new, before)]
    pallas_call x0 -> x3, Pallas kernels: none -> 77.4 us  [the longest x1 28.4 us: forward(): pl.pallas_call(forward_kernel, out_shape=jax.ShapeDtypeStruct((3, rows +...]
    reduce_sum x8 -> x0, other arithmetic: 19.6 us -> none  [the longest x4 12.8 us: block(): dist = jnp.sum(diff * diff, axis=0)]
    mul x7 -> x0, other arithmetic: 16.7 us -> none  [the longest x4 14.7 us: block(): (48.0 * inv_seven - 24.0 * inv_four) * cutoff * cutoff * weight[:, None, :]]
  transfers between devices with their start and end apart: 5 -> 0, of which waited for: 3 -> 0; matrix products, arithmetic and copies ran while one was open for 5% -> 0% of each run, Pallas kernels for 0% -> 0%
where the time goes in v1:
time: 86.2 us; the launch traced here: 84.5 us
  Pallas kernels  77.4 us (90%)
  local copies, waits for them, and re-layouts  5.71 us (7%)
  between operations  1.3 us (2%)
    pallas_call x1, Pallas kernels, forward(): pl.pallas_call(forward_kernel, out_shape=jax.ShapeDtypeStruct((3, rows +...  28.4 us
    pallas_call x1, Pallas kernels, forces(): pl.pallas_call(force_kernel, out_shape=jax.ShapeDtypeStruct((3, rows), F3...  27.6 us
    pallas_call x1, Pallas kernels, backward(): pl.pallas_call(backward_kernel, out_shape=(like, like), in_specs=[VM, VM,...  21.5 us
    unnamed x7, local copies, waits for them, and re-layouts  3.49 us
    pallas_call x2, local copies, waits for them, and re-layouts, backward(): pl.pallas_call(backward_kernel, out_shape=(like, like), in_specs=[VM, VM,...  2.21 us

profile of v1, /device:TPU:2, one launch (start us, length us, event | category | flops | bytes accessed | tf_op | source)
XLA Modules:
  0.0 84.5 jit_solution(16064330789197915669)
XLA Ops:
  1.3 1.4 %copy.8.neighbours = s32[1,32,8]{2,1,0:T(8,128)} copy(s32[1,32,8]{1,2,0:T(8,128)} %param.7) | data formatting | bytes 2048 | tf_op args[2]
  2.6 0.0 copy-start.1
  2.6 1.5 %copy.7.section = f32[1,3,4096]{2,1,0:T(4,128)} copy(f32[1,3,4096]{2,0,1:T(1,128)} %param.5) | data formatting | bytes 98304 | tf_op args[0]
  4.1 0.0 copy-done.1
  4.1 0.7 copy.10.momentum
  4.8 28.4 %forward_scan.1.ext = f32[3,5120]{1,0:T(4,128)} custom-call(f32[1,3,4096]{2,1,0:T(4,128)} %copy.7.section, s32[1,2,512]{2,1,0:T(2,128)} %border.1), custom_call_target="tpu_custom_call" | custom-call | tf_op jit(solution)/shard_map/forward_scan/pallas_call | solution.py:394
  33.1 27.6 %pair_forces.1.force = f32[3,4096]{1,0:T(4,128)} custom-call(s32[1]{0:T(128)S(6)} %copy.13.counts, s32[1,32,8]{2,1,0:T(8,128)} %copy.8.neighbours, f32[3,5120]{1,0:T(4,128)} %forward_scan.1.ext), custom_call_target="tpu_custom_call" | custom-call | tf_op jit(solution)/shard_map/pair_forces/pallas_call | solution.py:410
  60.7 21.5 %backward_scan.1 = (f32[1,3,4096]{2,1,0:T(4,128)}, f32[1,3,4096]{2,1,0:T(4,128)}) custom-call(f32[3,4096]{1,0:T(4,128)} %pair_forces.1.force, f32[1,3,4096]{2,1,0:T(4,128)} %copy.7.section, f32[1,3,4096]{2,1,0:T(4,128)} %copy.10.momentum), custom_call_target="tpu_custom_call" | custom-call | tf_op jit(solution)/shard_map/backward_scan/pallas_call | solution.py:428
  82.2 0.0 copy-start
  82.2 1.5 %copy.11 = f32[1,3,4096]{2,0,1:T(1,128)} copy(f32[1,3,4096]{2,1,0:T(4,128)} %get-tuple-element.2) | data formatting | bytes 98304 | tf_op jit(solution)/shard_map/backward_scan/pallas_call | solution.py:428
  83.8 0.0 copy-done
  83.8 0.7 copy.12
Async XLA Ops:
  2.6 1.5 %copy-start.1 = (f32[1,3,4096]{2,0,1:T(1,128)S(1)}, f32[1,3,4096]{2,0,1:T(1,128)}, u32[]{:S(2)}) copy-start(f32[1,3,4096]{2,0,1:T(1,128)} %param.6) | copy-start | bytes 147460
  82.2 1.6 %copy-start = (f32[1,3,4096]{2,1,0:T(4,128)S(1)}, f32[1,3,4096]{2,1,0:T(4,128)}, u32[]{:S(2)}) copy-start(f32[1,3,4096]{2,1,0:T(4,128)} %get-tuple-element.3) | copy-start | bytes 147460

commit v2 on v0

v2 whole, which is shorter than its diff:
```python
import functools
import math

import jax
import jax.numpy as jnp
from jax import lax
from jax.experimental import pallas as pl
from jax.experimental.pallas import tpu as pltpu
from jax.sharding import PartitionSpec as P

MESH = pl.DeviceIdType.MESH
time_step = 0.1
omega_sq = 4.0
slab_width = 3.0
reach_sq = 17.0
shrink = 1.0 / math.sqrt(reach_sq)
NX, NZ, NY = 4, 8, 2
TILE = 128
KROWS = 32
F32 = jnp.float32
BF16 = jnp.bfloat16
DMA = pltpu.SemaphoreType.DMA


def place():
    bead = lax.axis_index("bead")
    return bead // (NZ * NY), (bead // NY) % NZ, bead % NY


def bead_of(x, z, y):
    return (x * NZ + z) * NY + y


def to_bead(bead):
    return (bead, lax.axis_index("slab"))


def group_steps():
    return [(dz, dy) for dz in range(NZ) for dy in range(NY) if dz or dy]


def slab_peers():
    slab, count = lax.axis_index("slab"), lax.axis_size("slab")
    bead = lax.axis_index("bead")
    return (bead, (slab + 1) % count), (bead, (slab + count - 1) % count)


def partners():
    x, z, y = place()
    found = [to_bead(bead_of(x, (z + dz) % NZ, (y + dy) % NY)) for dz, dy in group_steps()]
    found += [to_bead(bead_of((x + dx) % NX, z, y)) for dx in range(1, NX)]
    return found + list(slab_peers())


def send(src, dst, send_sem, recv_sem, device):
    copy = pltpu.make_async_remote_copy(
        src_ref=src,
        dst_ref=dst,
        send_sem=send_sem,
        recv_sem=recv_sem,
        device_id=device,
        device_id_type=MESH,
    )
    copy.start()
    return copy


def scatter_chunks(chunk, r1, send_sem, recv_sem):
    x, z, y = place()
    copies = []
    for dz, dy in group_steps():
        tz = (z + dz) % NZ
        slot = dz * NY + dy
        device = to_bead(bead_of(x, tz, (y + dy) % NY))
        copies.append(send(chunk(tz), r1.at[slot], send_sem.at[slot], recv_sem.at[slot], device))
    return copies


def exchange_x(t2, r2, send_sem, recv_sem):
    x, z, y = place()
    return [
        send(t2, r2.at[dx], send_sem.at[dx], recv_sem.at[dx], to_bead(bead_of((x + dx) % NX, z, y)))
        for dx in range(1, NX)
    ]


def level_rows(bead):
    return jnp.full((1, 1, TILE), bead.astype(F32), F32)


def slot_from(zs, ys):
    x, z, y = place()
    return ((z + (NZ - zs)) % NZ) * NY + (y + (NY - ys)) % NY


def forward_scan(section, r1, t2, r2, px, land, sems):
    s1, q1, s2, q2, s3, q3 = sems
    x, z, y = place()
    sent = scatter_chunks(lambda c: section.at[:, c], r1, s1, q1)
    r1[0] = section[:, z]
    for copy in sent:
        copy.wait_recv()
    total = jnp.zeros(r1.shape[1:], F32)
    for zs in reversed(range(NZ)):
        kept = None
        for ys in reversed(range(NY)):
            level = level_rows(bead_of(x, zs, ys))
            inverse = jnp.where(level > 0, 1.0 / jnp.maximum(level, 1.0), 0.0)
            total = total + r1[slot_from(zs, ys)] * inverse
            kept = total if kept is None else jnp.where(y == ys, total, kept)
        px[zs] = kept
    first = r1[slot_from(0, 0)]
    t2[0] = total
    t2[1] = first
    swapped = exchange_x(t2, r2, s2, q2)
    for copy in swapped:
        copy.wait_recv()
    base = jnp.zeros(r1.shape[1:], F32)
    for dx in range(1, NX):
        xs = (x + (NX - dx)) % NX
        base = base + jnp.where(xs > x, r2[dx, 0], 0.0)
        first = jnp.where(xs == 0, r2[dx, 1], first)
    returned = []
    for dz in list(range(1, NZ)) + [0]:
        tz = (z + dz) % NZ
        level = level_rows(bead_of(x, tz, y))
        places = first + level * (px[tz] + base)
        if dz:
            px[tz] = places
            device = to_bead(bead_of(x, tz, y))
            returned.append(send(px.at[tz], land.at[1 + z], s3.at[dz], q3.at[dz], device))
        else:
            land[1 + z] = places
    for copy in returned:
        copy.wait_recv()
    return sent + swapped + returned


def backward_scan(force, r1, t2, r2, px, full, sems):
    s1, q1, s2, q2, s3, q3 = sems
    x, z, y = place()
    sent = scatter_chunks(lambda c: force.at[c], r1, s1, q1)
    r1[0] = force[z]
    for copy in sent:
        copy.wait_recv()
    total = jnp.zeros(r1.shape[1:], F32)
    plain = jnp.zeros(r1.shape[1:], F32)
    for zs in range(NZ):
        kept = None
        for ys in range(NY):
            one = r1[slot_from(zs, ys)]
            plain = plain + one
            total = total + one * level_rows(bead_of(x, zs, ys))
            kept = total if kept is None else jnp.where(y == ys, total, kept)
        px[zs] = kept
    t2[0] = total
    t2[1] = plain
    swapped = exchange_x(t2, r2, s2, q2)
    for copy in swapped:
        copy.wait_recv()
    base = jnp.zeros(r1.shape[1:], F32)
    for dx in range(1, NX):
        xs = (x + (NX - dx)) % NX
        base = base + jnp.where(xs < x, r2[dx, 0], 0.0)
        plain = plain + r2[dx, 1]
    returned = []
    for dz in list(range(1, NZ)) + [0]:
        tz = (z + dz) % NZ
        level = level_rows(bead_of(x, tz, y))
        inverse = 1.0 / jnp.maximum(level, 1.0)
        result = jnp.where(level > 0, (px[tz] + base) * inverse, plain)
        if dz:
            px[tz] = result
            device = to_bead(bead_of(x, tz, y))
            returned.append(send(px.at[tz], full.at[z], s3.at[dz], q3.at[dz], device))
        else:
            full[z] = result
    for copy in returned:
        copy.wait_recv()
    return sent + swapped + returned


def gather_rows(land, border, edge):
    tpc = land.shape[2]
    sub = lax.broadcasted_iota(jnp.int32, (8, TILE), 0)
    blocks = NZ // 2 * tpc // 8
    pieces = []
    for c in range(3):
        for b in range(blocks):
            rows = [land[1 + b * (8 // tpc) + m, c] for m in range(8 // tpc)]
            pieces.append(jnp.concatenate(rows, axis=0))
    for k in range(2):
        for n in range(tpc):
            index = jnp.broadcast_to(border[k : k + 1, n * TILE : (n + 1) * TILE], (8, TILE))
            lane, block = index % TILE, index // TILE
            for c in range(3):
                out = jnp.zeros((8, TILE), F32)
                for b in range(blocks):
                    taken = jnp.take_along_axis(
                        pieces[c * blocks + b], lane, axis=1, mode="promise_in_bounds"
                    )
                    out = jnp.where(block == b * 8 + sub, taken, out)
                edge[k, c, n : n + 1, :] = jnp.sum(out, axis=0, keepdims=True)


def halo_exchange(edge, land, send_sem, recv_sem):
    up_peer, down_peer = slab_peers()
    return [
        send(edge.at[0], land.at[0], send_sem.at[0], recv_sem.at[0], up_peer),
        send(edge.at[1], land.at[NZ + 1], send_sem.at[1], recv_sem.at[1], down_peer),
    ]


def split3(value):
    high = value.astype(BF16).astype(F32)
    rest = value - high
    middle = rest.astype(BF16).astype(F32)
    return high, middle, rest - middle


def prepare_tile(m, n, own, land, places, lefts, lefts_t, rights, centre_x, count):
    tpc = land.shape[2]
    t = m * tpc + n
    sub = lax.broadcasted_iota(jnp.int32, (8, TILE), 0)
    comp = sub % 4
    xs = [jnp.broadcast_to(land[m, c, pl.ds(n, 1), :], (8, TILE)) for c in range(3)]
    xs = [(v - w) * shrink for v, w in zip(xs, (centre_x, 0.5 * slab_width, 0.5 * slab_width))]
    p = jnp.where(comp == 0, xs[0], jnp.where(comp == 1, xs[1], xs[2]))
    norm = xs[0] * xs[0] + xs[1] * xs[1] + xs[2] * xs[2]
    if own:
        row = (t - tpc) * TILE + lax.broadcasted_iota(jnp.int32, (8, TILE), 1)
        far = jnp.where(row < count, norm, 4096.0)
    else:
        far = norm
    high, middle, low = split3(p)
    fh, fm, fl = split3(far)
    last, top = comp == 3, sub < 4
    a0 = jnp.where(last, jnp.where(top, fh, fm), high)
    a1 = jnp.where(last, jnp.where(top, fl, 1.0), middle)
    a2 = jnp.where(last, 1.0, jnp.where(top, low, high))
    left = jnp.concatenate([a0, a1, a2, jnp.zeros((8, TILE), F32)], axis=0)
    lefts[t] = left.astype(BF16)
    lefts_t[t] = left.T.astype(BF16)
    if own:
        nh, nm, nl = split3(norm + 1.0 / reach_sq)
        h2, m2, l2 = -2.0 * high, -2.0 * middle, -2.0 * low
        b0 = jnp.where(last, 1.0, jnp.where(top, h2, m2))
        b1 = jnp.where(last, jnp.where(top, 1.0, nh), jnp.where(top, h2, m2))
        b2 = jnp.where(last, jnp.where(top, nm, nl), jnp.where(top, h2, l2))
        right = jnp.concatenate([b0, b1, b2, jnp.zeros((8, TILE), F32)], axis=0)
        rights[t - tpc] = right.astype(BF16)
        places[t - tpc] = p


def prepare_chunk(m, own, *refs):
    tpc = refs[0].shape[2]
    for n in range(tpc):
        prepare_tile(m, n, own, *refs)


def quotients(i, buf, neighbours, lefts_t, rights):
    right = rights[i]
    for n in range(neighbours.shape[0]):
        buf[n * TILE : (n + 1) * TILE, :] = jnp.dot(
            lefts_t[neighbours[n, i]], right, preferred_element_type=F32
        )


def tile_force(i, buf, neighbours, lefts, places, force, count):
    tpc = force.shape[2]
    total = jnp.zeros((KROWS, TILE), F32)
    for n in range(0, neighbours.shape[0], 2):
        q = buf[n * TILE : (n + 2) * TILE, :]
        r = 1.0 / q
        r2 = r * r
        d = jnp.maximum(r2 - r, 0.0)
        f = ((d * d) * (r2 * r - 0.5 * reach_sq**3)).astype(BF16)
        x = jnp.concatenate([lefts[neighbours[n, i]], lefts[neighbours[n + 1, i]]], axis=1)
        total = total + jnp.dot(x, f, preferred_element_type=F32)
    moved = total[0:8] + total[8:16] + total[16:24]
    row = i * TILE + lax.broadcasted_iota(jnp.int32, (8, TILE), 1)
    beads = lax.axis_size("bead")
    scale = jnp.where(row < count, 48.0 / 256.0 / reach_sq**5 / shrink / beads, 0.0)
    result = (places[i] * total[15:16] - moved) * scale
    for c in range(3):
        force[i // tpc, c, pl.ds(i % tpc, 1), :] = result[c : c + 1]


def forces(neighbours, count, lefts, lefts_t, rights, places, even, odd, force):
    tiles = rights.shape[0]
    quotients(0, even, neighbours, lefts_t, rights)

    def pair(k, carry):
        i = 2 * k
        quotients(i + 1, odd, neighbours, lefts_t, rights)
        tile_force(i, even, neighbours, lefts, places, force, count)
        after = jnp.minimum(i + 2, tiles - 1)
        quotients(after, even, neighbours, lefts_t, rights)
        tile_force(i + 1, odd, neighbours, lefts, places, force, count)
        return carry

    lax.fori_loop(0, tiles // 2, pair, 0)


def leapfrog(section, momentum, full, new_section, new_momentum):
    level = level_rows(lax.axis_index("bead"))
    safe = jnp.maximum(level, 1.0)
    mass = jnp.where(level > 0, (level + 1.0) / safe, 1.0)
    spring = jnp.where(level > 0, omega_sq * mass, 0.0)
    step = time_step / 3.0
    push = 0.5 * step * spring
    drift = step / mass
    for z in range(NZ):
        p = momentum[:, z] + (0.5 * time_step) * full[z]
        u = section[:, z]
        for turn in range(3):
            p = p - push * u
            u = u + drift * p
            p = p - push * u
        new_section[:, z] = u
        new_momentum[:, z] = p


def kernel(
    counts, neighbours, border, section_in, momentum_in, section_out, momentum_out,
    section, momentum, result_u, result_p, land, edge, force, full,
    lefts, lefts_t, rights, places, even, odd,
    r1f, t2f, r2f, pxf, r1b, t2b, r2b, pxb,
    load_sem, store_sem, halo_send, halo_recv, *sems,
):
    slab, slabs = lax.axis_index("slab"), lax.axis_size("slab")
    loads = [
        pltpu.make_async_copy(section_in, section, load_sem.at[0]),
        pltpu.make_async_copy(momentum_in, momentum, load_sem.at[1]),
    ]
    for load in loads:
        load.start()
    barrier = pltpu.get_barrier_semaphore()
    greeted = partners()
    for device in greeted:
        pl.semaphore_signal(barrier, inc=1, device_id=device, device_id_type=MESH)
    pl.semaphore_wait(barrier, len(greeted))
    for load in loads:
        load.wait()
    started = forward_scan(section, r1f, t2f, r2f, pxf, land, sems[:6])
    gather_rows(land, border, edge)
    halos = halo_exchange(edge, land, halo_send, halo_recv)
    count = counts[0]
    box = slab_width * slabs
    centre = (slab.astype(F32) + 0.5) * slab_width
    refs = (land, places, lefts, lefts_t, rights)

    def own_chunk(m, carry):
        prepare_chunk(m, True, *refs, centre, count)
        return carry

    lax.fori_loop(1, NZ + 1, own_chunk, 0)
    for copy in halos:
        copy.wait_recv()
    prepare_chunk(0, False, *refs, centre + jnp.where(slab == 0, box, 0.0), count)
    prepare_chunk(NZ + 1, False, *refs, centre - jnp.where(slab == slabs - 1, box, 0.0), count)
    forces(neighbours, count, lefts, lefts_t, rights, places, even, odd, force)
    started += halos + backward_scan(force, r1b, t2b, r2b, pxb, full, sems[6:])
    leapfrog(section, momentum, full, result_u, result_p)
    stores = [
        pltpu.make_async_copy(result_u, section_out, store_sem.at[0]),
        pltpu.make_async_copy(result_p, momentum_out, store_sem.at[1]),
    ]
    for store in stores:
        store.start()
    for copy in started:
        copy.wait_send()
    for store in stores:
        store.wait()


def step(section, momentum, neighbours, border_rows, counts):
    shape = section.shape
    listed = neighbours.shape[2]
    tiles = shape[2] // TILE
    tpc = tiles // NZ
    dense = (3, NZ, tpc, TILE)
    ext_tiles = (NZ + 2) * tpc
    chunk = (3, tpc, TILE)
    anywhere = pl.BlockSpec(memory_space=pl.ANY)
    scan_buffers = [
        pltpu.VMEM((NZ * NY, *chunk), F32),
        pltpu.VMEM((2, *chunk), F32),
        pltpu.VMEM((NX, 2, *chunk), F32),
        pltpu.VMEM((NZ, *chunk), F32),
    ]
    scan_sems = [DMA((NZ * NY,))] * 2 + [DMA((NX,))] * 2 + [DMA((NZ,))] * 2
    like = jax.ShapeDtypeStruct(dense, F32)
    u, p = pl.pallas_call(
        kernel,
        out_shape=(like, like),
        in_specs=[
            pl.BlockSpec(memory_space=pltpu.SMEM),
            pl.BlockSpec(memory_space=pltpu.SMEM),
            pl.BlockSpec(memory_space=pltpu.VMEM),
            anywhere,
            anywhere,
        ],
        out_specs=(anywhere, anywhere),
        scratch_shapes=[pltpu.VMEM(dense, F32)] * 4
        + [
            pltpu.VMEM((NZ + 2, *chunk), F32),
            pltpu.VMEM((2, *chunk), F32),
            pltpu.VMEM((NZ, *chunk), F32),
            pltpu.VMEM((NZ, *chunk), F32),
            pltpu.VMEM((ext_tiles, KROWS, TILE), BF16),
            pltpu.VMEM((ext_tiles, TILE, KROWS), BF16),
            pltpu.VMEM((tiles, KROWS, TILE), BF16),
            pltpu.VMEM((tiles, 8, TILE), F32),
            pltpu.VMEM((listed * TILE, TILE), F32),
            pltpu.VMEM((listed * TILE, TILE), F32),
        ]
        + scan_buffers * 2
        + [DMA((2,))] * 4
        + scan_sems * 2,
        compiler_params=pltpu.CompilerParams(collective_id=0, has_side_effects=True),
        name="path_step",
    )(
        counts,
        neighbours.transpose(0, 2, 1).reshape(listed, tiles),
        border_rows.reshape(border_rows.shape[1:]),
        section.reshape(dense),
        momentum.reshape(dense),
    )
    return u.reshape(shape), p.reshape(shape)


def solution(mesh):
    return jax.shard_map(
        step,
        mesh=mesh,
        in_specs=(
            P("bead", None, "slab"),
            P("bead", None, "slab"),
            P("slab", None, None),
            P("slab", None, None),
            P("slab"),
        ),
        out_specs=(P("bead", None, "slab"), P("bead", None, "slab")),
        check_vma=False,
    )
```

time: 1250 us -> 57.8 us (0.05)
  waiting for transfers between devices: 718 us -> 0 us
  blocking collectives: 333 us -> 0 us
  other arithmetic: 161 us -> 0 us
  Pallas kernels: 0 us -> 53.3 us
  between operations: 14.6 us -> 1.29 us
    psum x1 -> x0, waiting for transfers between devices: 568 us -> none  [body(): total, weighted_total = lax.psum((bead_force, weighted), 'bead')]
    psum x1 -> x0, blocking collectives: 333 us -> none  [broadcast(): return lax.psum(jnp.where(mine, value, jnp.zeros_like(value)), axis)]
    all_gather x2 -> x0, waiting for transfers between devices: 147 us -> none  [prefix(): everything = lax.all_gather(value, axis)]
    select_n x136 -> x0, other arithmetic: 121 us -> none  [the longest x128 117 us: step(): return jnp.where(reached, new, before)]
    pallas_call x0 -> x1, Pallas kernels: none -> 53.3 us  [step(): pl.pallas_call(kernel, out_shape=(like, like), in_specs=[pl.BlockSpec(mem...]
    reduce_sum x8 -> x0, other arithmetic: 19.6 us -> none  [the longest x4 12.8 us: block(): dist = jnp.sum(diff * diff, axis=0)]
    mul x7 -> x0, other arithmetic: 16.7 us -> none  [the longest x4 14.7 us: block(): (48.0 * inv_seven - 24.0 * inv_four) * cutoff * cutoff * weight[:, None, :]]
  transfers between devices with their start and end apart: 5 -> 0, of which waited for: 3 -> 0; matrix products, arithmetic and copies ran while one was open for 5% -> 0% of each run, Pallas kernels for 0% -> 0%
where the time goes in v2:
time: 57.8 us; the launch traced here: 56.7 us
  Pallas kernels  53.3 us (92%)
  local copies, waits for them, and re-layouts  2.06 us (4%)
  between operations  1.29 us (2%)
    pallas_call x1, Pallas kernels, step(): pl.pallas_call(kernel, out_shape=(like, like), in_specs=[pl.BlockSpec(mem...  53.3 us
    unnamed x4, local copies, waits for them, and re-layouts  2.06 us

profile of v2, /device:TPU:2, one launch (start us, length us, event | category | flops | bytes accessed | tf_op | source)
XLA Modules:
  0.0 56.7 jit_solution(14674283986989960278)
XLA Ops:
  1.3 53.3 %path_step.1 = (f32[3,8,4,128]{3,2,1,0:T(4,128)}, f32[3,8,4,128]{3,2,1,0:T(4,128)}) custom-call(s32[1]{0:T(128)S(6)} %copy.13.counts, s32[8,32]{1,0:T(8,128)} %bitcast.12, s32[2,512]{1,0:T(2,128)} %bitcast.13, f32[3,8,4,128]{3,2,1,0:T(4,128)} %bitcast.10, f32[3,8,4,128]{3,2,1,0:T(4,128)} %bitcast.11), custom_call_target="tpu_custom_call" | custom-call | tf_op jit(solution)/shard_map/path_step/pallas_call | solution.py:394
  54.6 0.0 copy-start
  54.6 1.4 %copy.14 = f32[1,3,4096]{2,0,1:T(1,128)} copy(f32[1,3,4096]{2,0,1:T(1,128)} %bitcast.9) | data formatting | bytes 98304
  56.1 0.0 copy-done
  56.1 0.6 %copy.15 = f32[1,3,4096]{2,0,1:T(1,128)} copy(f32[1,3,4096]{2,0,1:T(1,128)S(1)} %bitcast.8) | data formatting | bytes 98304
Async XLA Ops:
  54.6 1.4 %copy-start = (f32[3,8,4,128]{3,2,1,0:T(4,128)S(1)}, f32[3,8,4,128]{3,2,1,0:T(4,128)}, u32[]{:S(2)}) copy-start(f32[3,8,4,128]{3,2,1,0:T(4,128)} %get-tuple-element.5) | copy-start | bytes 147460

commit v3 on v2

v3 whole, which is shorter than its diff:
```python
import functools
import math

import jax
import jax.numpy as jnp
from jax import lax
from jax.experimental import pallas as pl
from jax.experimental.pallas import tpu as pltpu
from jax.sharding import PartitionSpec as P

MESH = pl.DeviceIdType.MESH
time_step = 0.1
omega_sq = 4.0
slab_width = 3.0
reach_sq = 17.0
shrink = 1.0 / math.sqrt(reach_sq)
NX, NZ, NY = 4, 8, 2
TILE = 128
KROWS = 32
F32 = jnp.float32
BF16 = jnp.bfloat16
DMA = pltpu.SemaphoreType.DMA


def place():
    bead = lax.axis_index("bead")
    return bead // (NZ * NY), (bead // NY) % NZ, bead % NY


def bead_of(x, z, y):
    return (x * NZ + z) * NY + y


def to_bead(bead):
    return (bead, lax.axis_index("slab"))


def group_steps():
    return [(dz, dy) for dz in range(NZ) for dy in range(NY) if dz or dy]


def partners():
    x, z, y = place()
    slab, slabs = lax.axis_index("slab"), lax.axis_size("slab")
    found = [to_bead(bead_of(x, (z + dz) % NZ, (y + dy) % NY)) for dz, dy in group_steps()]
    found += [to_bead(bead_of((x + dx) % NX, z, y)) for dx in range(1, NX)]
    for ds in (1, slabs - 1):
        found += [(bead_of(x, (z + dz) % NZ, y), (slab + ds) % slabs) for dz in range(NZ)]
    return found


def send(src, dst, send_sem, recv_sem, device):
    copy = pltpu.make_async_remote_copy(
        src_ref=src,
        dst_ref=dst,
        send_sem=send_sem,
        recv_sem=recv_sem,
        device_id=device,
        device_id_type=MESH,
    )
    copy.start()
    return copy


def group_copy(src, r1, send_sem, recv_sem, dz, dy):
    x, z, y = place()
    slot = dz * NY + dy
    return pltpu.make_async_remote_copy(
        src_ref=src,
        dst_ref=r1.at[slot],
        send_sem=send_sem.at[slot],
        recv_sem=recv_sem.at[slot],
        device_id=to_bead(bead_of(x, (z + dz) % NZ, (y + dy) % NY)),
        device_id_type=MESH,
    )


def exchange_x(t2, r2, send_sem, recv_sem):
    x, z, y = place()
    return [
        send(t2, r2.at[dx], send_sem.at[dx], recv_sem.at[dx], to_bead(bead_of((x + dx) % NX, z, y)))
        for dx in range(1, NX)
    ]


def level_rows(bead):
    return jnp.full((1, TILE), bead.astype(F32), F32)


def slot_from(zs, ys):
    x, z, y = place()
    return ((z + (NZ - zs)) % NZ) * NY + (y + (NY - ys)) % NY


def near_first():
    return sorted(range(1, NZ), key=lambda dz: min(dz, NZ - dz))


def forward_scan(raw, r1, t2, r2, px, land, halo, sems):
    s1, q1, s2, q2, s3, q3, s4, q4 = sems
    x, z, y = place()
    slab, slabs = lax.axis_index("slab"), lax.axis_size("slab")
    sent = [group_copy(raw.at[(z + dz) % NZ], r1, s1, q1, dz, dy) for dz, dy in group_steps()]
    for copy in reversed(sent):
        copy.start()
    r1[0] = raw[z]
    for copy in sent:
        copy.wait_recv()
    total = jnp.zeros(r1.shape[1:], F32)
    for zs in reversed(range(NZ)):
        kept = None
        for ys in reversed(range(NY)):
            level = level_rows(bead_of(x, zs, ys))
            inverse = jnp.where(level > 0, 1.0 / jnp.maximum(level, 1.0), 0.0)
            total = total + r1[slot_from(zs, ys)] * inverse
            kept = total if kept is None else jnp.where(y == ys, total, kept)
        px[zs] = kept
    first = r1[slot_from(0, 0)]
    t2[0] = total
    t2[1] = first
    swapped = exchange_x(t2, r2, s2, q2)
    for copy in swapped:
        copy.wait_recv()
    base = jnp.zeros(r1.shape[1:], F32)
    for dx in range(1, NX):
        xs = (x + (NX - dx)) % NX
        base = base + jnp.where(xs > x, r2[dx, 0], 0.0)
        first = jnp.where(xs == 0, r2[dx, 1], first)
    beside = (slab + 1 + (slabs - 2) * (z // (NZ // 2))) % slabs
    returned, edges = [], []
    for dz in near_first()[::-1] + [0]:
        tz = (z + dz) % NZ
        bead = bead_of(x, tz, y)
        places = first + level_rows(bead) * (px[tz] + base)
        px[tz] = places
        edges.append(send(px.at[tz, 8:16], halo.at[z], s4.at[dz], q4.at[dz], (bead, beside)))
        if dz:
            returned.append(send(px.at[tz], land.at[z], s3.at[dz], q3.at[dz], to_bead(bead)))
        else:
            land[z] = places
    return sent + swapped, returned[::-1], edges[::-1]


def backward_scan(r1, t2, r2, px, full, arriving, sems):
    s2, q2, s3, q3 = sems
    x, z, y = place()
    for copy in arriving:
        copy.wait_recv()
    total = jnp.zeros(r1.shape[1:], F32)
    plain = jnp.zeros(r1.shape[1:], F32)
    for zs in range(NZ):
        kept = None
        for ys in range(NY):
            one = r1[slot_from(zs, ys)]
            plain = plain + one
            total = total + one * level_rows(bead_of(x, zs, ys))
            kept = total if kept is None else jnp.where(y == ys, total, kept)
        px[zs] = kept
    t2[0] = total
    t2[1] = plain
    swapped = exchange_x(t2, r2, s2, q2)
    for copy in swapped:
        copy.wait_recv()
    base = jnp.zeros(r1.shape[1:], F32)
    for dx in range(1, NX):
        xs = (x + (NX - dx)) % NX
        base = base + jnp.where(xs < x, r2[dx, 0], 0.0)
        plain = plain + r2[dx, 1]
    returned = []
    for dz in near_first()[::-1] + [0]:
        tz = (z + dz) % NZ
        bead = bead_of(x, tz, y)
        level = level_rows(bead)
        inverse = 1.0 / jnp.maximum(level, 1.0)
        result = jnp.where(level > 0, (px[tz] + base) * inverse, plain)
        if dz:
            px[tz] = result
            returned.append(send(px.at[tz], full.at[z], s3.at[dz], q3.at[dz], to_bead(bead)))
        else:
            full[z] = result
    return swapped, returned[::-1]


def pack_chunks(section, border, raw):
    tpc = section.shape[2]
    sub = lax.broadcasted_iota(jnp.int32, (8, TILE), 0)
    blocks = NZ // 2 * tpc // 8
    for z in range(NZ):
        for c in range(3):
            raw[z, c * tpc : (c + 1) * tpc, :] = section[c, z]
    pieces = []
    for c in range(3):
        for b in range(blocks):
            rows = [section[c, b * (8 // tpc) + m] for m in range(8 // tpc)]
            pieces.append(jnp.concatenate(rows, axis=0))
    half = NZ // 2
    for z in range(NZ):
        k, n = z // half, z % half
        index = jnp.broadcast_to(border[k : k + 1, n * TILE : (n + 1) * TILE], (8, TILE))
        lane, block = index % TILE, index // TILE
        rows = []
        for c in range(3):
            out = jnp.zeros((8, TILE), F32)
            for b in range(blocks):
                taken = jnp.take_along_axis(
                    pieces[c * blocks + b], lane, axis=1, mode="promise_in_bounds"
                )
                out = jnp.where(block == b * 8 + sub, taken, out)
            rows.append(jnp.sum(out, axis=0, keepdims=True))
        raw[z, 12:16, :] = jnp.concatenate(rows + [jnp.zeros((1, TILE), F32)], axis=0)


def split3(value):
    high = value.astype(BF16).astype(F32)
    rest = value - high
    middle = rest.astype(BF16).astype(F32)
    return high, middle, rest - middle


def prepare_tile(t, rows, shift, own, lefts, lefts_t, rights, places, row, count):
    sub = lax.broadcasted_iota(jnp.int32, (8, TILE), 0)
    comp = sub % 4
    xs = [jnp.broadcast_to(v, (8, TILE)) for v in rows]
    xs = [(v - w) * shrink for v, w in zip(xs, (shift, 0.5 * slab_width, 0.5 * slab_width))]
    p = jnp.where(comp == 0, xs[0], jnp.where(comp == 1, xs[1], xs[2]))
    norm = xs[0] * xs[0] + xs[1] * xs[1] + xs[2] * xs[2]
    far = norm
    if own is not None:
        place_in = row + lax.broadcasted_iota(jnp.int32, (8, TILE), 1)
        far = jnp.where(place_in < count, norm, 4096.0)
    high, middle, low = split3(p)
    fh, fm, fl = split3(far)
    last, top = comp == 3, sub < 4
    a0 = jnp.where(last, jnp.where(top, fh, fm), high)
    a1 = jnp.where(last, jnp.where(top, fl, 1.0), middle)
    a2 = jnp.where(last, 1.0, jnp.where(top, low, high))
    left = jnp.concatenate([a0, a1, a2, jnp.zeros((8, TILE), F32)], axis=0)
    lefts[t] = left.astype(BF16)
    lefts_t[t] = left.T.astype(BF16)
    if own is not None:
        nh, nm, nl = split3(norm + 1.0 / reach_sq)
        h2, m2, l2 = -2.0 * high, -2.0 * middle, -2.0 * low
        b0 = jnp.where(last, 1.0, jnp.where(top, h2, m2))
        b1 = jnp.where(last, jnp.where(top, 1.0, nh), jnp.where(top, h2, m2))
        b2 = jnp.where(last, jnp.where(top, nm, nl), jnp.where(top, h2, l2))
        right = jnp.concatenate([b0, b1, b2, jnp.zeros((8, TILE), F32)], axis=0)
        rights[own] = right.astype(BF16)
        places[own] = p


def prepare_own(z, land, centre, count, *refs):
    half, tpc = NZ // 2, refs[2].shape[0] // NZ
    for n in range(tpc):
        rows = [land[z, c * tpc + n : c * tpc + n + 1, :] for c in range(3)]
        i = z * tpc + n
        prepare_tile(half + i, rows, centre, i, *refs, i * TILE, count)


def prepare_halo(z, halo, shifts, *refs):
    half, tiles = NZ // 2, refs[2].shape[0]
    upper = z // half
    rows = [halo[z, 4 + c : 5 + c, :] for c in range(3)]
    shift = jnp.where(upper == 0, shifts[0], shifts[1])
    prepare_tile(z + upper * tiles, rows, shift, None, *refs, 0, 0)


def quotients(i, buf, neighbours, lefts_t, rights):
    right = rights[i]
    for n in range(neighbours.shape[0]):
        buf[n * TILE : (n + 1) * TILE, :] = jnp.dot(
            lefts_t[neighbours[n, i]], right, preferred_element_type=F32
        )


def tile_force(i, zc, n, buf, neighbours, lefts, places, force, count):
    total = jnp.zeros((KROWS, TILE), F32)
    for k in range(0, neighbours.shape[0], 2):
        q = buf[k * TILE : (k + 2) * TILE, :]
        r = 1.0 / q
        r2 = r * r
        d = jnp.maximum(r2 - r, 0.0)
        f = ((d * d) * (r2 * r - 0.5 * reach_sq**3)).astype(BF16)
        x = jnp.concatenate([lefts[neighbours[k, i]], lefts[neighbours[k + 1, i]]], axis=1)
        total = total + jnp.dot(x, f, preferred_element_type=F32)
    moved = total[0:8] + total[8:16] + total[16:24]
    row = i * TILE + lax.broadcasted_iota(jnp.int32, (8, TILE), 1)
    beads = lax.axis_size("bead")
    scale = jnp.where(row < count, 48.0 / 256.0 / reach_sq**5 / shrink / beads, 0.0)
    result = (places[i] * total[15:16] - moved) * scale
    for c in range(3):
        force[zc, 4 * c + n : 4 * c + n + 1, :] = result[c : c + 1]


def forces(neighbours, count, lefts, lefts_t, rights, places, even, odd, force, r1, send_sem, recv_sem):
    x, z, y = place()
    tpc = rights.shape[0] // NZ
    half = NZ // 2
    bufs = (even, odd)

    def offset(c):
        return half + (c // 2) * (1 - c % 2) - ((c + 1) // 2) * (c % 2)

    quotients(((z + half) % NZ) * tpc, even, neighbours, lefts_t, rights)

    def chunk(c, carry):
        dz = offset(c)
        zc = (z + dz) % NZ
        after = (z + offset(jnp.minimum(c + 1, NZ - 1))) % NZ
        for n in range(tpc):
            following = zc * tpc + n + 1 if n + 1 < tpc else after * tpc
            quotients(following, bufs[(n + 1) % 2], neighbours, lefts_t, rights)
            tile_force(zc * tpc + n, zc, n, bufs[n % 2], neighbours, lefts, places, force, count)
        group_copy(force.at[zc], r1, send_sem, recv_sem, dz, 1).start()

        @pl.when(c < NZ - 1)
        def _():
            group_copy(force.at[zc], r1, send_sem, recv_sem, dz, 0).start()

        return carry

    lax.fori_loop(0, NZ, chunk, 0)
    r1[0] = force[z]
    return [group_copy(force.at[(z + dz) % NZ], r1, send_sem, recv_sem, dz, dy) for dz, dy in group_steps()]


def kernel(
    counts, neighbours, border, section_in, out,
    section, result, raw, land, halo, force, full,
    lefts, lefts_t, rights, places, even, odd,
    r1f, t2f, r2f, pxf, r1b, t2b, r2b, pxb,
    load_sem, store_sem, *sems,
):
    x, z, y = place()
    slab, slabs = lax.axis_index("slab"), lax.axis_size("slab")
    load = pltpu.make_async_copy(section_in, section, load_sem.at[0])
    load.start()
    barrier = pltpu.get_barrier_semaphore()
    greeted = partners()
    for device in greeted:
        pl.semaphore_signal(barrier, inc=1, device_id=device, device_id_type=MESH)
    force[...] = jnp.zeros_like(force)
    load.wait()
    pack_chunks(section, border, raw)
    pl.semaphore_wait(barrier, len(greeted))
    started, returned, edges = forward_scan(raw, r1f, t2f, r2f, pxf, land, halo, sems[:8])
    count = counts[0]
    box = slab_width * slabs
    centre = (slab.astype(F32) + 0.5) * slab_width
    shifts = (
        centre + jnp.where(slab == 0, box, 0.0),
        centre - jnp.where(slab == slabs - 1, box, 0.0),
    )
    refs = (lefts, lefts_t, rights, places)
    prepare_own(z, land, centre, count, *refs)
    for copy, edge, dz in zip([None] + returned, edges, [0] + near_first()):
        source = (z + (NZ - dz)) % NZ
        if copy is not None:
            copy.wait_recv()
            prepare_own(source, land, centre, count, *refs)
        edge.wait_recv()
        prepare_halo(source, halo, shifts, *refs)
    arriving = forces(
        neighbours, count, lefts, lefts_t, rights, places, even, odd, force, r1b, *sems[8:10]
    )
    swapped, back = backward_scan(r1b, t2b, r2b, pxb, full, arriving, sems[10:])
    tpc = result.shape[2]
    for copy, dz in zip([None] + back, [0] + near_first()):
        source = (z + (NZ - dz)) % NZ
        if copy is not None:
            copy.wait_recv()
        for c in range(3):
            result[c, source] = full[source, c * tpc : (c + 1) * tpc, :]
    store = pltpu.make_async_copy(result, out, store_sem.at[0])
    store.start()
    for copy in started + returned + edges + arriving + swapped + back:
        copy.wait_send()
    store.wait()


def leapfrog(section, momentum, section_force):
    level = lax.axis_index("bead").astype(F32)
    safe = jnp.maximum(level, 1.0)
    mass = jnp.where(level > 0, (level + 1.0) / safe, 1.0)
    spring = jnp.where(level > 0, omega_sq * mass, 0.0)
    step = time_step / 3.0
    push = 0.5 * step * spring
    drift = step / mass
    p = momentum + (0.5 * time_step) * section_force
    u = section
    for turn in range(3):
        p = p - push * u
        u = u + drift * p
        p = p - push * u
    return u, p


def step(section, momentum, neighbours, border_rows, counts):
    shape = section.shape
    listed = neighbours.shape[2]
    tiles = shape[2] // TILE
    tpc = tiles // NZ
    dense = (3, NZ, tpc, TILE)
    ext_tiles = tiles + NZ
    chunk = (16, TILE)
    anywhere = pl.BlockSpec(memory_space=pl.ANY)
    vmem = lambda *dims: pltpu.VMEM(dims, F32)
    scan_buffers = [vmem(NZ * NY, *chunk), vmem(2, *chunk), vmem(NX, 2, *chunk), vmem(NZ, *chunk)]
    scan_sems = [DMA((NZ * NY,))] * 2 + [DMA((NX,))] * 2 + [DMA((NZ,))] * 2
    section, momentum = section.reshape(dense), momentum.reshape(dense)
    section_force = pl.pallas_call(
        kernel,
        out_shape=jax.ShapeDtypeStruct(dense, F32),
        in_specs=[
            pl.BlockSpec(memory_space=pltpu.SMEM),
            pl.BlockSpec(memory_space=pltpu.SMEM),
            pl.BlockSpec(memory_space=pltpu.VMEM),
            anywhere,
        ],
        out_specs=anywhere,
        scratch_shapes=[
            vmem(*dense),
            vmem(*dense),
            vmem(NZ, *chunk),
            vmem(NZ, *chunk),
            vmem(NZ, 8, TILE),
            vmem(NZ, *chunk),
            vmem(NZ, *chunk),
            pltpu.VMEM((ext_tiles, KROWS, TILE), BF16),
            pltpu.VMEM((ext_tiles, TILE, KROWS), BF16),
            pltpu.VMEM((tiles, KROWS, TILE), BF16),
            vmem(tiles, 8, TILE),
            vmem(listed * TILE, TILE),
            vmem(listed * TILE, TILE),
        ]
        + scan_buffers * 2
        + [DMA((1,))] * 2
        + scan_sems
        + [DMA((NZ,))] * 2
        + scan_sems,
        compiler_params=pltpu.CompilerParams(
            collective_id=0, has_side_effects=True, vmem_limit_bytes=24 * 2**20
        ),
        name="path_step",
    )(
        counts,
        neighbours.transpose(0, 2, 1).reshape(listed, tiles),
        border_rows.reshape(border_rows.shape[1:]),
        section,
    )
    u, p = leapfrog(section, momentum, section_force)
    return u.reshape(shape), p.reshape(shape)


def solution(mesh):
    return jax.shard_map(
        step,
        mesh=mesh,
        in_specs=(
            P("bead", None, "slab"),
            P("bead", None, "slab"),
            P("slab", None, None),
            P("slab", None, None),
            P("slab"),
        ),
        out_specs=(P("bead", None, "slab"), P("bead", None, "slab")),
        check_vma=False,
    )
```

time: 57.8 us -> 50.1 us (0.87); the launches traced: 56.7 us -> 49.7 us
  Pallas kernels: 53.3 us -> 46.1 us
  other arithmetic: 0 us -> 0.71 us
  local copies, waits for them, and re-layouts: 2.06 us -> 1.48 us
    pallas_call x1, Pallas kernels: 53.3 us -> 46.1 us  [step(): pl.pallas_call(kernel, out_shape=jax.ShapeDtypeStruct(dense, F32), in_spe...]
    sub x0 -> x1, other arithmetic: none -> 0.71 us  [leapfrog(): p = p - push * u]
    unnamed x4 -> x8, local copies, waits for them, and re-layouts: 2.06 us -> 1.48 us
where the time goes in v3:
time: 50.1 us; the launch traced here: 49.7 us
  Pallas kernels  46.1 us (92%)
  local copies, waits for them, and re-layouts  1.48 us (3%)
  between operations  1.42 us (3%)
  other arithmetic  0.71 us (1%)
    pallas_call x1, Pallas kernels, step(): pl.pallas_call(kernel, out_shape=jax.ShapeDtypeStruct(dense, F32), in_spe...  46.1 us
    unnamed x8, local copies, waits for them, and re-layouts  1.48 us

profile of v3, /device:TPU:2, one launch (start us, length us, event | category | flops | bytes accessed | tf_op | source)
XLA Modules:
  0.0 49.7 jit_solution(14046680119801897987)
XLA Ops:
  0.7 0.0 copy-start.2
  1.4 0.0 copy-start.1
  1.4 0.0 copy-done.2
  1.4 0.7 %copy-done.1 = s32[1,32,8]{1,2,0:T(8,128)S(1)} copy-done((s32[1,32,8]{1,2,0:T(8,128)S(1)}, s32[1,32,8]{1,2,0:T(8,128)}, u32[]{:S(2)}) %copy-start.1) | copy-done | bytes 1048
  2.1 0.0 copy-start
  2.1 0.8 %copy-done = f32[1,3,4096]{2,0,1:T(1,128)S(1)} copy-done((f32[1,3,4096]{2,0,1:T(1,128)S(1)}, f32[1,3,4096]{2,0,1:T(1,128)}, u32[]{:S(2)}) %copy-start) | copy-done | bytes 49176
  2.9 0.0 copy-start.3
  2.9 46.1 %path_step.1 = f32[3,8,4,128]{3,2,1,0:T(4,128)S(1)} custom-call(s32[1]{0:T(128)S(6)} %copy.11.counts, s32[8,32]{1,0:T(8,128)S(1)} %bitcast.10, s32[2,512]{1,0:T(2,128)S(1)} %bitcast.11, f32[3,8,4,128]{3,2,1,0:T(4,128)S(1)} %bitcast.8), custom_call_target="tpu_custom_call" | custom-call | tf_op jit(solution)/shard_map/path_step/pallas_call | solution.py:410
  49.0 0.0 copy-done.3
  49.0 0.7 %multiply_subtract_fusion = (f32[3,8,4,128]{3,2,1,0:T(4,128)}, f32[3,8,4,128]{3,2,1,0:T(4,128)}) fusion(f32[]{:T(128)S(6)} %mul_shard_map.7, f32[3,8,4,128]{3,2,1,0:T(4,128)S(1)} %bitcast.9, f32[]{:T(128)S(6)} %div.7, f32[3,8,4,128]{3,2,1,0:T(4,128)S(1)} %bitcast.12, f32[3,8,4,128]{3,2,1,0:T(4,128)S(1)} %path_step.1), kind=kLoop, calls=%fused_computation.2 | loop fusion | flops 221184 | bytes 245768 | tf_op jit(solution)/shard_map/sub | solution.py:393
Async XLA Ops:
  0.7 0.7 %copy-start.2 = (s32[1,2,512]{2,1,0:T(2,128)S(1)}, s32[1,2,512]{2,1,0:T(2,128)}, u32[]{:S(2)}) copy-start(s32[1,2,512]{2,1,0:T(2,128)} %param.8) | copy-start | bytes 12292
  1.4 0.7 %copy-start.1 = (s32[1,32,8]{1,2,0:T(8,128)S(1)}, s32[1,32,8]{1,2,0:T(8,128)}, u32[]{:S(2)}) copy-start(s32[1,32,8]{1,2,0:T(8,128)} %param.7) | copy-start | bytes 3076
  2.1 0.8 %copy-start = (f32[1,3,4096]{2,0,1:T(1,128)S(1)}, f32[1,3,4096]{2,0,1:T(1,128)}, u32[]{:S(2)}) copy-start(f32[1,3,4096]{2,0,1:T(1,128)} %param.5) | copy-start | bytes 147460
  2.9 46.1 %copy-start.3 = (f32[1,3,4096]{2,0,1:T(1,128)S(1)}, f32[1,3,4096]{2,0,1:T(1,128)}, u32[]{:S(2)}) copy-start(f32[1,3,4096]{2,0,1:T(1,128)} %param.6) | copy-start | bytes 147460

commit v4 on v3

--- a/solution.py
+++ b/solution.py
@@ -324,22 +324,28 @@
 
 
 def kernel(
-    counts, neighbours, border, section_in, out,
-    section, result, raw, land, halo, force, full,
+    counts, neighbours_in, border_in, section_in, out,
+    neighbours, border, section, result, raw, land, halo, force, full,
     lefts, lefts_t, rights, places, even, odd,
     r1f, t2f, r2f, pxf, r1b, t2b, r2b, pxb,
     load_sem, store_sem, *sems,
 ):
     x, z, y = place()
     slab, slabs = lax.axis_index("slab"), lax.axis_size("slab")
-    load = pltpu.make_async_copy(section_in, section, load_sem.at[0])
-    load.start()
+    loads = [
+        pltpu.make_async_copy(section_in, section, load_sem.at[0]),
+        pltpu.make_async_copy(border_in, border, load_sem.at[1]),
+        pltpu.make_async_copy(neighbours_in, neighbours, load_sem.at[2]),
+    ]
+    for load in loads:
+        load.start()
     barrier = pltpu.get_barrier_semaphore()
     greeted = partners()
     for device in greeted:
         pl.semaphore_signal(barrier, inc=1, device_id=device, device_id_type=MESH)
     force[...] = jnp.zeros_like(force)
-    load.wait()
+    for load in loads:
+        load.wait()
     pack_chunks(section, border, raw)
     pl.semaphore_wait(barrier, len(greeted))
     started, returned, edges = forward_scan(raw, r1f, t2f, r2f, pxf, land, halo, sems[:8])
@@ -364,17 +370,20 @@
     )
     swapped, back = backward_scan(r1b, t2b, r2b, pxb, full, arriving, sems[10:])
     tpc = result.shape[2]
+    stores = []
     for copy, dz in zip([None] + back, [0] + near_first()):
         source = (z + (NZ - dz)) % NZ
         if copy is not None:
             copy.wait_recv()
         for c in range(3):
             result[c, source] = full[source, c * tpc : (c + 1) * tpc, :]
-    store = pltpu.make_async_copy(result, out, store_sem.at[0])
-    store.start()
+        store = pltpu.make_async_copy(result.at[:, source], out.at[:, source], store_sem.at[dz])
+        store.start()
+        stores.append(store)
     for copy in started + returned + edges + arriving + swapped + back:
         copy.wait_send()
-    store.wait()
+    for store in stores:
+        store.wait()
 
 
 def leapfrog(section, momentum, section_force):
@@ -403,6 +412,8 @@
     ext_tiles = tiles + NZ
     chunk = (16, TILE)
     anywhere = pl.BlockSpec(memory_space=pl.ANY)
+    in_hbm = pl.BlockSpec(memory_space=pltpu.HBM)
+    hbm = lambda array: pltpu.with_memory_space_constraint(array, pltpu.HBM)
     vmem = lambda *dims: pltpu.VMEM(dims, F32)
     scan_buffers = [vmem(NZ * NY, *chunk), vmem(2, *chunk), vmem(NX, 2, *chunk), vmem(NZ, *chunk)]
     scan_sems = [DMA((NZ * NY,))] * 2 + [DMA((NX,))] * 2 + [DMA((NZ,))] * 2
@@ -412,12 +423,14 @@
         out_shape=jax.ShapeDtypeStruct(dense, F32),
         in_specs=[
             pl.BlockSpec(memory_space=pltpu.SMEM),
-            pl.BlockSpec(memory_space=pltpu.SMEM),
-            pl.BlockSpec(memory_space=pltpu.VMEM),
-            anywhere,
+            in_hbm,
+            in_hbm,
+            in_hbm,
         ],
         out_specs=anywhere,
         scratch_shapes=[
+            pltpu.SMEM((listed, tiles), jnp.int32),
+            pltpu.VMEM(border_rows.shape[1:], jnp.int32),
             vmem(*dense),
             vmem(*dense),
             vmem(NZ, *chunk),
@@ -433,7 +446,7 @@
             vmem(listed * TILE, TILE),
         ]
         + scan_buffers * 2
-        + [DMA((1,))] * 2
+        + [DMA((3,)), DMA((NZ,))]
         + scan_sems
         + [DMA((NZ,))] * 2
         + scan_sems,
@@ -443,9 +456,9 @@
         name="path_step",
     )(
         counts,
-        neighbours.transpose(0, 2, 1).reshape(listed, tiles),
-        border_rows.reshape(border_rows.shape[1:]),
-        section,
+        hbm(neighbours.transpose(0, 2, 1).reshape(listed, tiles)),
+        hbm(border_rows.reshape(border_rows.shape[1:])),
+        hbm(section),
     )
     u, p = leapfrog(section, momentum, section_force)
     return u.reshape(shape), p.reshape(shape)

time: 50.1 us -> 48.2 us (0.962)
  local copies, waits for them, and re-layouts: 1.48 us -> 0.01 us
    unnamed x8 -> x4, local copies, waits for them, and re-layouts: 1.48 us -> 0.01 us
where the time goes in v4:
time: 48.2 us; the launch traced here: 47.7 us
  Pallas kernels  45.6 us (95%)
  between operations  1.41 us (3%)
  other arithmetic  0.71 us (1%)
    pallas_call x1, Pallas kernels, step(): pl.pallas_call(kernel, out_shape=jax.ShapeDtypeStruct(dense, F32), in_spe...  45.6 us

profile of v4, /device:TPU:2, one launch (start us, length us, event | category | flops | bytes accessed | tf_op | source)
XLA Modules:
  0.0 47.7 jit_solution(633709545429835707)
XLA Ops:
  1.4 0.0 copy-start
  1.4 0.0 copy-start.1
  1.4 45.6 %path_step.1 = f32[3,8,4,128]{3,2,1,0:T(4,128)S(1)} custom-call(s32[1]{0:T(128)S(6)} %copy.11.counts, s32[8,32]{1,0:T(8,128)} %bitcast.13, s32[2,512]{1,0:T(2,128)} %bitcast.14, f32[3,8,4,128]{3,2,1,0:T(4,128)} %bitcast.8), custom_call_target="tpu_custom_call" | custom-call | tf_op jit(solution)/shard_map/path_step/pallas_call | solution.py:421
  47.0 0.0 copy-done
  47.0 0.0 copy-done.1
  47.0 0.7 %multiply_subtract_fusion = (f32[3,8,4,128]{3,2,1,0:T(4,128)}, f32[3,8,4,128]{3,2,1,0:T(4,128)}) fusion(f32[]{:T(128)S(6)} %mul_shard_map.7, f32[3,8,4,128]{3,2,1,0:T(4,128)S(1)} %bitcast.9, f32[]{:T(128)S(6)} %div.7, f32[3,8,4,128]{3,2,1,0:T(4,128)S(1)} %bitcast.10, f32[3,8,4,128]{3,2,1,0:T(4,128)S(1)} %path_step.1), kind=kLoop, calls=%fused_computation.2 | loop fusion | flops 221184 | bytes 245768 | tf_op jit(solution)/shard_map/sub | solution.py:402
Async XLA Ops:
  1.4 45.6 %copy-start = (f32[1,3,4096]{2,0,1:T(1,128)S(1)}, f32[1,3,4096]{2,0,1:T(1,128)}, u32[]{:S(2)}) copy-start(f32[1,3,4096]{2,0,1:T(1,128)} %param.5) | copy-start | bytes 147460
  1.4 45.6 %copy-start.1 = (f32[1,3,4096]{2,0,1:T(1,128)S(1)}, f32[1,3,4096]{2,0,1:T(1,128)}, u32[]{:S(2)}) copy-start(f32[1,3,4096]{2,0,1:T(1,128)} %param.6) | copy-start | bytes 147460

commit v5 on v4

--- a/solution.py
+++ b/solution.py
@@ -22,9 +22,13 @@
 DMA = pltpu.SemaphoreType.DMA
 
 
+def rem(value, size):
+    return lax.rem(value, jnp.int32(size))
+
+
 def place():
     bead = lax.axis_index("bead")
-    return bead // (NZ * NY), (bead // NY) % NZ, bead % NY
+    return lax.div(bead, jnp.int32(NZ * NY)), rem(lax.div(bead, jnp.int32(NY)), NZ), rem(bead, NY)
 
 
 def bead_of(x, z, y):
@@ -42,10 +46,10 @@
 def partners():
     x, z, y = place()
     slab, slabs = lax.axis_index("slab"), lax.axis_size("slab")
-    found = [to_bead(bead_of(x, (z + dz) % NZ, (y + dy) % NY)) for dz, dy in group_steps()]
-    found += [to_bead(bead_of((x + dx) % NX, z, y)) for dx in range(1, NX)]
+    found = [to_bead(bead_of(x, rem(z + dz, NZ), rem(y + dy, NY))) for dz, dy in group_steps()]
+    found += [to_bead(bead_of(rem(x + dx, NX), z, y)) for dx in range(1, NX)]
     for ds in (1, slabs - 1):
-        found += [(bead_of(x, (z + dz) % NZ, y), (slab + ds) % slabs) for dz in range(NZ)]
+        found += [(bead_of(x, rem(z + dz, NZ), y), rem(slab + ds, slabs)) for dz in range(NZ)]
     return found
 
 
@@ -70,7 +74,7 @@
         dst_ref=r1.at[slot],
         send_sem=send_sem.at[slot],
         recv_sem=recv_sem.at[slot],
-        device_id=to_bead(bead_of(x, (z + dz) % NZ, (y + dy) % NY)),
+        device_id=to_bead(bead_of(x, rem(z + dz, NZ), rem(y + dy, NY))),
         device_id_type=MESH,
     )
 
@@ -78,18 +82,18 @@
 def exchange_x(t2, r2, send_sem, recv_sem):
     x, z, y = place()
     return [
-        send(t2, r2.at[dx], send_sem.at[dx], recv_sem.at[dx], to_bead(bead_of((x + dx) % NX, z, y)))
+        send(t2, r2.at[pl.ds(2 * dx, 2)], send_sem.at[dx], recv_sem.at[dx], to_bead(bead_of(rem(x + dx, NX), z, y)))
         for dx in range(1, NX)
     ]
 
 
 def level_rows(bead):
-    return jnp.full((1, TILE), bead.astype(F32), F32)
+    return jnp.full((1, 1, TILE), bead.astype(F32), F32)
 
 
 def slot_from(zs, ys):
     x, z, y = place()
-    return ((z + (NZ - zs)) % NZ) * NY + (y + (NY - ys)) % NY
+    return rem(z + (NZ - zs), NZ) * NY + rem(y + (NY - ys), NY)
 
 
 def near_first():
@@ -100,7 +104,7 @@
     s1, q1, s2, q2, s3, q3, s4, q4 = sems
     x, z, y = place()
     slab, slabs = lax.axis_index("slab"), lax.axis_size("slab")
-    sent = [group_copy(raw.at[(z + dz) % NZ], r1, s1, q1, dz, dy) for dz, dy in group_steps()]
+    sent = [group_copy(raw.at[rem(z + dz, NZ)], r1, s1, q1, dz, dy) for dz, dy in group_steps()]
     for copy in reversed(sent):
         copy.start()
     r1[0] = raw[z]
@@ -110,9 +114,10 @@
     for zs in reversed(range(NZ)):
         kept = None
         for ys in reversed(range(NY)):
-            level = level_rows(bead_of(x, zs, ys))
-            inverse = jnp.where(level > 0, 1.0 / jnp.maximum(level, 1.0), 0.0)
-            total = total + r1[slot_from(zs, ys)] * inverse
+            one = r1[slot_from(zs, ys)]
+            if zs == 0 and ys == 0:
+                one = jnp.where(x == 0, 0.0, one)
+            total = total + one
             kept = total if kept is None else jnp.where(y == ys, total, kept)
         px[zs] = kept
     first = r1[slot_from(0, 0)]
@@ -123,21 +128,21 @@
         copy.wait_recv()
     base = jnp.zeros(r1.shape[1:], F32)
     for dx in range(1, NX):
-        xs = (x + (NX - dx)) % NX
-        base = base + jnp.where(xs > x, r2[dx, 0], 0.0)
-        first = jnp.where(xs == 0, r2[dx, 1], first)
-    beside = (slab + 1 + (slabs - 2) * (z // (NZ // 2))) % slabs
+        xs = rem(x + (NX - dx), NX)
+        base = base + jnp.where(xs > x, r2[2 * dx], 0.0)
+        first = jnp.where(xs == 0, r2[2 * dx + 1], first)
+    beside = rem(slab + 1 + (slabs - 2) * lax.div(z, jnp.int32(NZ // 2)), slabs)
     returned, edges = [], []
     for dz in near_first()[::-1] + [0]:
-        tz = (z + dz) % NZ
+        tz = rem(z + dz, NZ)
         bead = bead_of(x, tz, y)
         places = first + level_rows(bead) * (px[tz] + base)
         px[tz] = places
-        edges.append(send(px.at[tz, 8:16], halo.at[z], s4.at[dz], q4.at[dz], (bead, beside)))
+        edges.append(send(px.at[tz, 3], halo.at[z], s4.at[dz], q4.at[dz], (bead, beside)))
         if dz:
-            returned.append(send(px.at[tz], land.at[z], s3.at[dz], q3.at[dz], to_bead(bead)))
+            returned.append(send(px.at[tz, 0:3], land.at[z], s3.at[dz], q3.at[dz], to_bead(bead)))
         else:
-            land[z] = places
+            land[z] = places[0:3]
     return sent + swapped, returned[::-1], edges[::-1]
 
 
@@ -163,16 +168,14 @@
         copy.wait_recv()
     base = jnp.zeros(r1.shape[1:], F32)
     for dx in range(1, NX):
-        xs = (x + (NX - dx)) % NX
-        base = base + jnp.where(xs < x, r2[dx, 0], 0.0)
-        plain = plain + r2[dx, 1]
+        xs = rem(x + (NX - dx), NX)
+        base = base + jnp.where(xs < x, r2[2 * dx], 0.0)
+        plain = plain + r2[2 * dx + 1]
     returned = []
     for dz in near_first()[::-1] + [0]:
-        tz = (z + dz) % NZ
+        tz = rem(z + dz, NZ)
         bead = bead_of(x, tz, y)
-        level = level_rows(bead)
-        inverse = 1.0 / jnp.maximum(level, 1.0)
-        result = jnp.where(level > 0, (px[tz] + base) * inverse, plain)
+        result = jnp.where(bead > 0, px[tz] + base, plain)
         if dz:
             px[tz] = result
             returned.append(send(px.at[tz], full.at[z], s3.at[dz], q3.at[dz], to_bead(bead)))
@@ -182,12 +185,13 @@
 
 
 def pack_chunks(section, border, raw):
+    level = level_rows(lax.axis_index("bead"))
+    inverse = 1.0 / jnp.maximum(level, 1.0)
     tpc = section.shape[2]
     sub = lax.broadcasted_iota(jnp.int32, (8, TILE), 0)
     blocks = NZ // 2 * tpc // 8
     for z in range(NZ):
-        for c in range(3):
-            raw[z, c * tpc : (c + 1) * tpc, :] = section[c, z]
+        raw[z, 0:3] = section[:, z] * inverse
     pieces = []
     for c in range(3):
         for b in range(blocks):
@@ -207,7 +211,7 @@
                 )
                 out = jnp.where(block == b * 8 + sub, taken, out)
             rows.append(jnp.sum(out, axis=0, keepdims=True))
-        raw[z, 12:16, :] = jnp.concatenate(rows + [jnp.zeros((1, TILE), F32)], axis=0)
+        raw[z, 3] = jnp.concatenate(rows + [jnp.zeros((1, TILE), F32)], axis=0) * inverse[0]
 
 
 def split3(value):
@@ -251,15 +255,15 @@
 def prepare_own(z, land, centre, count, *refs):
     half, tpc = NZ // 2, refs[2].shape[0] // NZ
     for n in range(tpc):
-        rows = [land[z, c * tpc + n : c * tpc + n + 1, :] for c in range(3)]
+        rows = [land[z, c, n : n + 1, :] for c in range(3)]
         i = z * tpc + n
         prepare_tile(half + i, rows, centre, i, *refs, i * TILE, count)
 
 
 def prepare_halo(z, halo, shifts, *refs):
     half, tiles = NZ // 2, refs[2].shape[0]
-    upper = z // half
-    rows = [halo[z, 4 + c : 5 + c, :] for c in range(3)]
+    upper = lax.div(z, jnp.int32(half))
+    rows = [halo[z, c : c + 1, :] for c in range(3)]
     shift = jnp.where(upper == 0, shifts[0], shifts[1])
     prepare_tile(z + upper * tiles, rows, shift, None, *refs, 0, 0)
 
@@ -288,7 +292,7 @@
     scale = jnp.where(row < count, 48.0 / 256.0 / reach_sq**5 / shrink / beads, 0.0)
     result = (places[i] * total[15:16] - moved) * scale
     for c in range(3):
-        force[zc, 4 * c + n : 4 * c + n + 1, :] = result[c : c + 1]
+        force[zc, c, n : n + 1, :] = result[c : c + 1]
 
 
 def forces(neighbours, count, lefts, lefts_t, rights, places, even, odd, force, r1, send_sem, recv_sem):
@@ -298,14 +302,14 @@
     bufs = (even, odd)
 
     def offset(c):
-        return half + (c // 2) * (1 - c % 2) - ((c + 1) // 2) * (c % 2)
-
-    quotients(((z + half) % NZ) * tpc, even, neighbours, lefts_t, rights)
+        return half + lax.div(c, jnp.int32(2)) * (1 - rem(c, 2)) - lax.div(c + 1, jnp.int32(2)) * rem(c, 2)
+
+    quotients(rem(z + half, NZ) * tpc, even, neighbours, lefts_t, rights)
 
     def chunk(c, carry):
         dz = offset(c)
-        zc = (z + dz) % NZ
-        after = (z + offset(jnp.minimum(c + 1, NZ - 1))) % NZ
+        zc = rem(z + dz, NZ)
+        after = rem(z + offset(jnp.minimum(c + 1, NZ - 1)), NZ)
         for n in range(tpc):
             following = zc * tpc + n + 1 if n + 1 < tpc else after * tpc
             quotients(following, bufs[(n + 1) % 2], neighbours, lefts_t, rights)
@@ -320,12 +324,12 @@
 
     lax.fori_loop(0, NZ, chunk, 0)
     r1[0] = force[z]
-    return [group_copy(force.at[(z + dz) % NZ], r1, send_sem, recv_sem, dz, dy) for dz, dy in group_steps()]
+    return [group_copy(force.at[rem(z + dz, NZ)], r1, send_sem, recv_sem, dz, dy) for dz, dy in group_steps()]
 
 
 def kernel(
     counts, neighbours_in, border_in, section_in, out,
-    neighbours, border, section, result, raw, land, halo, force, full,
+    neighbours, border, section, raw, land, halo, force, full,
     lefts, lefts_t, rights, places, even, odd,
     r1f, t2f, r2f, pxf, r1b, t2b, r2b, pxb,
     load_sem, store_sem, *sems,
@@ -343,7 +347,6 @@
     greeted = partners()
     for device in greeted:
         pl.semaphore_signal(barrier, inc=1, device_id=device, device_id_type=MESH)
-    force[...] = jnp.zeros_like(force)
     for load in loads:
         load.wait()
     pack_chunks(section, border, raw)
@@ -359,7 +362,7 @@
     refs = (lefts, lefts_t, rights, places)
     prepare_own(z, land, centre, count, *refs)
     for copy, edge, dz in zip([None] + returned, edges, [0] + near_first()):
-        source = (z + (NZ - dz)) % NZ
+        source = rem(z + (NZ - dz), NZ)
         if copy is not None:
             copy.wait_recv()
             prepare_own(source, land, centre, count, *refs)
@@ -369,15 +372,12 @@
         neighbours, count, lefts, lefts_t, rights, places, even, odd, force, r1b, *sems[8:10]
     )
     swapped, back = backward_scan(r1b, t2b, r2b, pxb, full, arriving, sems[10:])
-    tpc = result.shape[2]
     stores = []
     for copy, dz in zip([None] + back, [0] + near_first()):
-        source = (z + (NZ - dz)) % NZ
+        source = rem(z + (NZ - dz), NZ)
         if copy is not None:
             copy.wait_recv()
-        for c in range(3):
-            result[c, source] = full[source, c * tpc : (c + 1) * tpc, :]
-        store = pltpu.make_async_copy(result.at[:, source], out.at[:, source], store_sem.at[dz])
+        store = pltpu.make_async_copy(full.at[source], out.at[:, source], store_sem.at[dz])
         store.start()
         stores.append(store)
     for copy in started + returned + edges + arriving + swapped + back:
@@ -389,6 +389,7 @@
 def leapfrog(section, momentum, section_force):
     level = lax.axis_index("bead").astype(F32)
     safe = jnp.maximum(level, 1.0)
+    section_force = section_force / safe
     mass = jnp.where(level > 0, (level + 1.0) / safe, 1.0)
     spring = jnp.where(level > 0, omega_sq * mass, 0.0)
     step = time_step / 3.0
@@ -410,12 +411,16 @@
     tpc = tiles // NZ
     dense = (3, NZ, tpc, TILE)
     ext_tiles = tiles + NZ
-    chunk = (16, TILE)
+    chunk, wide = (3, tpc, TILE), (4, tpc, TILE)
     anywhere = pl.BlockSpec(memory_space=pl.ANY)
     in_hbm = pl.BlockSpec(memory_space=pltpu.HBM)
     hbm = lambda array: pltpu.with_memory_space_constraint(array, pltpu.HBM)
     vmem = lambda *dims: pltpu.VMEM(dims, F32)
-    scan_buffers = [vmem(NZ * NY, *chunk), vmem(2, *chunk), vmem(NX, 2, *chunk), vmem(NZ, *chunk)]
+    scan_buffers = [
+        vmem(count, *part)
+        for part in (wide, chunk)
+        for count in (NZ * NY, 2, NX * 2, NZ)
+    ]
     scan_sems = [DMA((NZ * NY,))] * 2 + [DMA((NX,))] * 2 + [DMA((NZ,))] * 2
     section, momentum = section.reshape(dense), momentum.reshape(dense)
     section_force = pl.pallas_call(
@@ -432,10 +437,9 @@
             pltpu.SMEM((listed, tiles), jnp.int32),
             pltpu.VMEM(border_rows.shape[1:], jnp.int32),
             vmem(*dense),
-            vmem(*dense),
+            vmem(NZ, *wide),
             vmem(NZ, *chunk),
-            vmem(NZ, *chunk),
-            vmem(NZ, 8, TILE),
+            vmem(NZ, 4, TILE),
             vmem(NZ, *chunk),
             vmem(NZ, *chunk),
             pltpu.VMEM((ext_tiles, KROWS, TILE), BF16),
@@ -445,7 +449,7 @@
             vmem(listed * TILE, TILE),
             vmem(listed * TILE, TILE),
         ]
-        + scan_buffers * 2
+        + scan_buffers
         + [DMA((3,)), DMA((NZ,))]
         + scan_sems
         + [DMA((NZ,))] * 2

time: 48.2 us -> 47.7 us (0.990)
  no operation moved by 1% of the time
where the time goes in v5:
time: 47.7 us; the launch traced here: 47.4 us
  Pallas kernels  45.3 us (95%)
  between operations  1.41 us (3%)
  other arithmetic  0.71 us (1%)
    pallas_call x1, Pallas kernels, step(): pl.pallas_call(kernel, out_shape=jax.ShapeDtypeStruct(dense, F32), in_spe...  45.3 us

profile of v5, /device:TPU:2, one launch (start us, length us, event | category | flops | bytes accessed | tf_op | source)
XLA Modules:
  0.0 47.4 jit_solution(9857188916229816639)
XLA Ops:
  1.4 0.0 copy-start
  1.4 0.0 copy-start.1
  1.4 45.3 %path_step.1 = f32[3,8,4,128]{3,2,1,0:T(4,128)S(1)} custom-call(s32[1]{0:T(128)S(6)} %copy.11.counts, s32[8,32]{1,0:T(8,128)} %bitcast.13, s32[2,512]{1,0:T(2,128)} %bitcast.14, f32[3,8,4,128]{3,2,1,0:T(4,128)} %bitcast.8), custom_call_target="tpu_custom_call" | custom-call | tf_op jit(solution)/shard_map/path_step/pallas_call | solution.py:426
  46.7 0.0 copy-done
  46.7 0.0 copy-done.1
  46.7 0.7 %multiply_subtract_fusion = (f32[3,8,4,128]{3,2,1,0:T(4,128)}, f32[3,8,4,128]{3,2,1,0:T(4,128)}) fusion(f32[]{:T(128)S(6)} %mul_shard_map.7, f32[3,8,4,128]{3,2,1,0:T(4,128)S(1)} %bitcast.9, f32[]{:T(128)S(6)} %div.13, f32[3,8,4,128]{3,2,1,0:T(4,128)S(1)} %bitcast.10, f32[3,8,4,128]{3,2,1,0:T(4,128)S(1)} %path_step.1, f32[]{:T(128)S(6)} %max.3), kind=kLoop, calls=%fused_computation.2 | loop fusion | flops 233472 | bytes 245772 | tf_op jit(solution)/shard_map/sub | solution.py:403
Async XLA Ops:
  1.4 45.3 %copy-start = (f32[1,3,4096]{2,0,1:T(1,128)S(1)}, f32[1,3,4096]{2,0,1:T(1,128)}, u32[]{:S(2)}) copy-start(f32[1,3,4096]{2,0,1:T(1,128)} %param.5) | copy-start | bytes 147460
  1.4 45.3 %copy-start.1 = (f32[1,3,4096]{2,0,1:T(1,128)S(1)}, f32[1,3,4096]{2,0,1:T(1,128)}, u32[]{:S(2)}) copy-start(f32[1,3,4096]{2,0,1:T(1,128)} %param.6) | copy-start | bytes 147460

commit v6 on v5

--- a/solution.py
+++ b/solution.py
@@ -43,18 +43,23 @@
     return [(dz, dy) for dz in range(NZ) for dy in range(NY) if dz or dy]
 
 
+def reach(dz):
+    return min(dz, NZ - dz)
+
+
 def partners():
     x, z, y = place()
     slab, slabs = lax.axis_index("slab"), lax.axis_size("slab")
-    found = [to_bead(bead_of(x, rem(z + dz, NZ), rem(y + dy, NY))) for dz, dy in group_steps()]
-    found += [to_bead(bead_of(rem(x + dx, NX), z, y)) for dx in range(1, NX)]
-    for ds in (1, slabs - 1):
-        found += [(bead_of(x, rem(z + dz, NZ), y), rem(slab + ds, slabs)) for dz in range(NZ)]
-    return found
-
-
-def send(src, dst, send_sem, recv_sem, device):
-    copy = pltpu.make_async_remote_copy(
+    found = []
+    for dz in sorted(range(NZ), key=reach, reverse=True):
+        tz = rem(z + dz, NZ)
+        found += [to_bead(bead_of(x, tz, rem(y + dy, NY))) for dy in reversed(range(NY)) if dz or dy]
+        found += [(bead_of(x, tz, y), rem(slab + ds, slabs)) for ds in (1, slabs - 1)]
+    return found + [to_bead(bead_of(rem(x + dx, NX), z, y)) for dx in range(1, NX)]
+
+
+def remote(src, dst, send_sem, recv_sem, device):
+    return pltpu.make_async_remote_copy(
         src_ref=src,
         dst_ref=dst,
         send_sem=send_sem,
@@ -62,29 +67,29 @@
         device_id=device,
         device_id_type=MESH,
     )
+
+
+def send(*args):
+    copy = remote(*args)
     copy.start()
     return copy
 
 
+def await_bytes(ref, sem):
+    pltpu.make_async_copy(ref, ref, sem).wait()
+
+
 def group_copy(src, r1, send_sem, recv_sem, dz, dy):
     x, z, y = place()
-    slot = dz * NY + dy
-    return pltpu.make_async_remote_copy(
-        src_ref=src,
-        dst_ref=r1.at[slot],
-        send_sem=send_sem.at[slot],
-        recv_sem=recv_sem.at[slot],
-        device_id=to_bead(bead_of(x, rem(z + dz, NZ), rem(y + dy, NY))),
-        device_id_type=MESH,
-    )
-
-
-def exchange_x(t2, r2, send_sem, recv_sem):
-    x, z, y = place()
-    return [
-        send(t2, r2.at[pl.ds(2 * dx, 2)], send_sem.at[dx], recv_sem.at[dx], to_bead(bead_of(rem(x + dx, NX), z, y)))
-        for dx in range(1, NX)
-    ]
+    device = to_bead(bead_of(x, rem(z + dz, NZ), rem(y + dy, NY)))
+    return remote(src, r1.at[dz * NY + dy], send_sem.at[0], recv_sem.at[0], device)
+
+
+def exchange_x(src, slots, send_sem, recv_sem):
+    x, z, y = place()
+    for dx in range(1, NX):
+        device = to_bead(bead_of(rem(x + dx, NX), z, y))
+        send(src, slots.at[dx], send_sem.at[0], recv_sem.at[0], device)
 
 
 def level_rows(bead):
@@ -97,19 +102,25 @@
 
 
 def near_first():
-    return sorted(range(1, NZ), key=lambda dz: min(dz, NZ - dz))
-
-
-def forward_scan(raw, r1, t2, r2, px, land, halo, sems):
-    s1, q1, s2, q2, s3, q3, s4, q4 = sems
+    return sorted(range(1, NZ), key=reach)
+
+
+def forward_scan(raw, r1, t2, r2, first_in, px, land, halo, sems):
+    s1, q1, s2, q2, sf, qf, s3, q3, s4, q4 = sems
     x, z, y = place()
     slab, slabs = lax.axis_index("slab"), lax.axis_size("slab")
-    sent = [group_copy(raw.at[rem(z + dz, NZ)], r1, s1, q1, dz, dy) for dz, dy in group_steps()]
-    for copy in reversed(sent):
-        copy.start()
+    for dz, dy in reversed(group_steps()):
+        group_copy(raw.at[rem(z + dz, NZ)], r1, s1, q1, dz, dy).start()
     r1[0] = raw[z]
-    for copy in sent:
-        copy.wait_recv()
+    await_bytes(r1.at[1:], q1.at[0])
+
+    @pl.when(x == 0)
+    def _():
+        for dx in range(1, NX):
+            device = to_bead(bead_of(dx, z, y))
+            send(r1.at[slot_from(0, 0)], first_in.at[0], sf.at[0], qf.at[0], device)
+        first_in[0] = r1[slot_from(0, 0)]
+
     total = jnp.zeros(r1.shape[1:], F32)
     for zs in reversed(range(NZ)):
         kept = None
@@ -120,39 +131,50 @@
             total = total + one
             kept = total if kept is None else jnp.where(y == ys, total, kept)
         px[zs] = kept
-    first = r1[slot_from(0, 0)]
     t2[0] = total
-    t2[1] = first
-    swapped = exchange_x(t2, r2, s2, q2)
-    for copy in swapped:
-        copy.wait_recv()
+    exchange_x(t2.at[0], r2, s2, q2)
+
+    @pl.when(x != 0)
+    def _():
+        await_bytes(first_in.at[0], qf.at[0])
+
+    await_bytes(r2.at[1:], q2.at[0])
     base = jnp.zeros(r1.shape[1:], F32)
     for dx in range(1, NX):
         xs = rem(x + (NX - dx), NX)
-        base = base + jnp.where(xs > x, r2[2 * dx], 0.0)
-        first = jnp.where(xs == 0, r2[2 * dx + 1], first)
+        base = base + jnp.where(xs > x, r2[dx], 0.0)
+    first = first_in[0]
     beside = rem(slab + 1 + (slabs - 2) * lax.div(z, jnp.int32(NZ // 2)), slabs)
-    returned, edges = [], []
     for dz in near_first()[::-1] + [0]:
         tz = rem(z + dz, NZ)
         bead = bead_of(x, tz, y)
         places = first + level_rows(bead) * (px[tz] + base)
         px[tz] = places
-        edges.append(send(px.at[tz, 3], halo.at[z], s4.at[dz], q4.at[dz], (bead, beside)))
+        send(px.at[tz, 3], halo.at[z], s4.at[0], q4.at[dz], (bead, beside))
         if dz:
-            returned.append(send(px.at[tz, 0:3], land.at[z], s3.at[dz], q3.at[dz], to_bead(bead)))
+            send(px.at[tz, 0:3], land.at[z], s3.at[0], q3.at[dz], to_bead(bead))
         else:
             land[z] = places[0:3]
-    return sent + swapped, returned[::-1], edges[::-1]
-
-
-def backward_scan(r1, t2, r2, px, full, arriving, sems):
-    s2, q2, s3, q3 = sems
-    x, z, y = place()
-    for copy in arriving:
-        copy.wait_recv()
+
+    def finish():
+        await_bytes(r1.at[1:], s1.at[0])
+        await_bytes(r2.at[1:], s2.at[0])
+        await_bytes(land.at[1:], s3.at[0])
+        await_bytes(halo, s4.at[0])
+
+        @pl.when(x == 0)
+        def _():
+            await_bytes(r2.at[1:], sf.at[0])
+
+    return finish
+
+
+def backward_scan(r1, t2, r2, plain_in, px, out, sems):
+    s1, q1, s2, q2, sf, qf, s3, q3, own_sem = sems
+    x, z, y = place()
+    await_bytes(r1.at[1:], q1.at[0])
+    plain = jnp.zeros(r1.shape[1:], F32)
     total = jnp.zeros(r1.shape[1:], F32)
-    plain = jnp.zeros(r1.shape[1:], F32)
     for zs in range(NZ):
         kept = None
         for ys in range(NY):
@@ -163,25 +185,50 @@
         px[zs] = kept
     t2[0] = total
     t2[1] = plain
-    swapped = exchange_x(t2, r2, s2, q2)
-    for copy in swapped:
-        copy.wait_recv()
+    exchange_x(t2.at[0], r2, s2, q2)
+
+    @pl.when(x != 0)
+    def _():
+        send(t2.at[1], plain_in.at[x], sf.at[0], qf.at[0], to_bead(bead_of(0, z, y)))
+
+    @pl.when(x == 0)
+    def _():
+        plain_in[0] = plain
+        await_bytes(plain_in.at[1:], qf.at[0])
+
+    await_bytes(r2.at[1:], q2.at[0])
     base = jnp.zeros(r1.shape[1:], F32)
     for dx in range(1, NX):
         xs = rem(x + (NX - dx), NX)
-        base = base + jnp.where(xs < x, r2[2 * dx], 0.0)
-        plain = plain + r2[2 * dx + 1]
-    returned = []
+        base = base + jnp.where(xs < x, r2[dx], 0.0)
+    for zs in range(NZ):
+        px[zs] = px[zs] + base
+
+    @pl.when((x == 0) & (y == 0))
+    def _():
+        everything = plain_in[0]
+        for xs in range(1, NX):
+            everything = everything + plain_in[xs]
+        px[0] = everything
+
     for dz in near_first()[::-1] + [0]:
         tz = rem(z + dz, NZ)
-        bead = bead_of(x, tz, y)
-        result = jnp.where(bead > 0, px[tz] + base, plain)
         if dz:
-            px[tz] = result
-            returned.append(send(px.at[tz], full.at[z], s3.at[dz], q3.at[dz], to_bead(bead)))
+            device = to_bead(bead_of(x, tz, y))
+            send(px.at[tz], out.at[:, z], s3.at[0], q3.at[0], device)
         else:
-            full[z] = result
-    return swapped, returned[::-1]
+            own = pltpu.make_async_copy(px.at[tz], out.at[:, z], own_sem.at[0])
+            own.start()
+
+    await_bytes(px.at[1:], q3.at[0])
+    own.wait()
+    await_bytes(r1.at[1:], s1.at[0])
+    await_bytes(r2.at[1:], s2.at[0])
+    await_bytes(px.at[1:], s3.at[0])
+
+    @pl.when(x != 0)
+    def _():
+        await_bytes(t2.at[1], sf.at[0])
 
 
 def pack_chunks(section, border, raw):
@@ -324,15 +371,14 @@
 
     lax.fori_loop(0, NZ, chunk, 0)
     r1[0] = force[z]
-    return [group_copy(force.at[rem(z + dz, NZ)], r1, send_sem, recv_sem, dz, dy) for dz, dy in group_steps()]
 
 
 def kernel(
     counts, neighbours_in, border_in, section_in, out,
-    neighbours, border, section, raw, land, halo, force, full,
+    neighbours, border, section, raw, land, halo, force,
     lefts, lefts_t, rights, places, even, odd,
-    r1f, t2f, r2f, pxf, r1b, t2b, r2b, pxb,
-    load_sem, store_sem, *sems,
+    r1f, t2f, r2f, first_in, pxf, r1b, t2b, r2b, plain_in, pxb,
+    load_sem, *sems,
 ):
     x, z, y = place()
     slab, slabs = lax.axis_index("slab"), lax.axis_size("slab")
@@ -351,7 +397,8 @@
         load.wait()
     pack_chunks(section, border, raw)
     pl.semaphore_wait(barrier, len(greeted))
-    started, returned, edges = forward_scan(raw, r1f, t2f, r2f, pxf, land, halo, sems[:8])
+    finish = forward_scan(raw, r1f, t2f, r2f, first_in, pxf, land, halo, sems[:10])
+    q3, q4 = sems[7], sems[9]
     count = counts[0]
     box = slab_width * slabs
     centre = (slab.astype(F32) + 0.5) * slab_width
@@ -360,30 +407,26 @@
         centre - jnp.where(slab == slabs - 1, box, 0.0),
     )
     refs = (lefts, lefts_t, rights, places)
-    prepare_own(z, land, centre, count, *refs)
-    for copy, edge, dz in zip([None] + returned, edges, [0] + near_first()):
-        source = rem(z + (NZ - dz), NZ)
-        if copy is not None:
-            copy.wait_recv()
-            prepare_own(source, land, centre, count, *refs)
-        edge.wait_recv()
-        prepare_halo(source, halo, shifts, *refs)
-    arriving = forces(
-        neighbours, count, lefts, lefts_t, rights, places, even, odd, force, r1b, *sems[8:10]
+    farthest = NZ // 2
+    for distance in range(farthest + 1):
+        chunks = [dz for dz in range(NZ) if reach(dz) == distance]
+        tiles = [dz for dz in range(NZ) if reach(dz) == distance - 1]
+        if distance == farthest:
+            tiles += chunks
+        for dz in chunks:
+            if dz:
+                await_bytes(land.at[0], q3.at[dz])
+        for dz in tiles:
+            await_bytes(halo.at[0], q4.at[dz])
+        for dz in chunks:
+            prepare_own(rem(z + (NZ - dz), NZ), land, centre, count, *refs)
+        for dz in tiles:
+            prepare_halo(rem(z + (NZ - dz), NZ), halo, shifts, *refs)
+    forces(
+        neighbours, count, lefts, lefts_t, rights, places, even, odd, force, r1b, sems[10], sems[11]
     )
-    swapped, back = backward_scan(r1b, t2b, r2b, pxb, full, arriving, sems[10:])
-    stores = []
-    for copy, dz in zip([None] + back, [0] + near_first()):
-        source = rem(z + (NZ - dz), NZ)
-        if copy is not None:
-            copy.wait_recv()
-        store = pltpu.make_async_copy(full.at[source], out.at[:, source], store_sem.at[dz])
-        store.start()
-        stores.append(store)
-    for copy in started + returned + edges + arriving + swapped + back:
-        copy.wait_send()
-    for store in stores:
-        store.wait()
+    backward_scan(r1b, t2b, r2b, plain_in, pxb, out, sems[10:])
+    finish()
 
 
 def leapfrog(section, momentum, section_force):
@@ -419,9 +462,9 @@
     scan_buffers = [
         vmem(count, *part)
         for part in (wide, chunk)
-        for count in (NZ * NY, 2, NX * 2, NZ)
+        for count in (NZ * NY, 2, NX, NX, NZ)
     ]
-    scan_sems = [DMA((NZ * NY,))] * 2 + [DMA((NX,))] * 2 + [DMA((NZ,))] * 2
+    one, each = DMA((1,)), DMA((NZ,))
     section, momentum = section.reshape(dense), momentum.reshape(dense)
     section_force = pl.pallas_call(
         kernel,
@@ -441,7 +484,6 @@
             vmem(NZ, *chunk),
             vmem(NZ, 4, TILE),
             vmem(NZ, *chunk),
-            vmem(NZ, *chunk),
             pltpu.VMEM((ext_tiles, KROWS, TILE), BF16),
             pltpu.VMEM((ext_tiles, TILE, KROWS), BF16),
             pltpu.VMEM((tiles, KROWS, TILE), BF16),
@@ -450,10 +492,10 @@
             vmem(listed * TILE, TILE),
         ]
         + scan_buffers
-        + [DMA((3,)), DMA((NZ,))]
-        + scan_sems
-        + [DMA((NZ,))] * 2
-        + scan_sems,
+        + [DMA((3,))]
+        + [one] * 6
+        + [one, each] * 2
+        + [one] * 9,
         compiler_params=pltpu.CompilerParams(
             collective_id=0, has_side_effects=True, vmem_limit_bytes=24 * 2**20
         ),

time: 47.7 us -> 46.1 us (0.966)
  Pallas kernels: 45.3 us -> 43.8 us
    pallas_call x1, Pallas kernels: 45.3 us -> 43.8 us  [step(): pl.pallas_call(kernel, out_shape=jax.ShapeDtypeStruct(dense, F32), in_spe...]
where the time goes in v6:
time: 46.1 us; the launch traced here: 45.9 us
  Pallas kernels  43.8 us (95%)
  between operations  1.41 us (3%)
  other arithmetic  0.71 us (2%)
    pallas_call x1, Pallas kernels, step(): pl.pallas_call(kernel, out_shape=jax.ShapeDtypeStruct(dense, F32), in_spe...  43.8 us

profile of v6, /device:TPU:2, one launch (start us, length us, event | category | flops | bytes accessed | tf_op | source)
XLA Modules:
  0.0 45.9 jit_solution(9268920476894532078)
XLA Ops:
  1.4 0.0 copy-start
  1.4 0.0 copy-start.1
  1.4 43.8 %path_step.1 = f32[3,8,4,128]{3,2,1,0:T(4,128)S(1)} custom-call(s32[1]{0:T(128)S(6)} %copy.11.counts, s32[8,32]{1,0:T(8,128)} %bitcast.13, s32[2,512]{1,0:T(2,128)} %bitcast.14, f32[3,8,4,128]{3,2,1,0:T(4,128)} %bitcast.8), custom_call_target="tpu_custom_call" | custom-call | tf_op jit(solution)/shard_map/path_step/pallas_call | solution.py:469
  45.2 0.0 copy-done
  45.2 0.0 copy-done.1
  45.2 0.7 %multiply_subtract_fusion = (f32[3,8,4,128]{3,2,1,0:T(4,128)}, f32[3,8,4,128]{3,2,1,0:T(4,128)}) fusion(f32[]{:T(128)S(6)} %mul_shard_map.7, f32[3,8,4,128]{3,2,1,0:T(4,128)S(1)} %bitcast.9, f32[]{:T(128)S(6)} %div.13, f32[3,8,4,128]{3,2,1,0:T(4,128)S(1)} %bitcast.10, f32[3,8,4,128]{3,2,1,0:T(4,128)S(1)} %path_step.1, f32[]{:T(128)S(6)} %max.3), kind=kLoop, calls=%fused_computation.2 | loop fusion | flops 233472 | bytes 245772 | tf_op jit(solution)/shard_map/sub | solution.py:446
Async XLA Ops:
  1.4 43.8 %copy-start = (f32[1,3,4096]{2,0,1:T(1,128)S(1)}, f32[1,3,4096]{2,0,1:T(1,128)}, u32[]{:S(2)}) copy-start(f32[1,3,4096]{2,0,1:T(1,128)} %param.5) | copy-start | bytes 147460
  1.4 43.8 %copy-start.1 = (f32[1,3,4096]{2,0,1:T(1,128)S(1)}, f32[1,3,4096]{2,0,1:T(1,128)}, u32[]{:S(2)}) copy-start(f32[1,3,4096]{2,0,1:T(1,128)} %param.6) | copy-start | bytes 147460

commit v7 on v6

--- a/solution.py
+++ b/solution.py
@@ -79,10 +79,22 @@
     pltpu.make_async_copy(ref, ref, sem).wait()
 
 
-def group_copy(src, r1, send_sem, recv_sem, dz, dy):
+def group_copy(src, r1, send_sem, recv_sem, dz, dy, kind=0):
     x, z, y = place()
     device = to_bead(bead_of(x, rem(z + dz, NZ), rem(y + dy, NY)))
-    return remote(src, r1.at[dz * NY + dy], send_sem.at[0], recv_sem.at[0], device)
+    return remote(src, r1.at[dz * NY + dy], send_sem.at[0], recv_sem.at[kind], device)
+
+
+def near_offsets():
+    return (1, NZ - 1, 0)
+
+
+def near_slots():
+    return [(dx, k, dy) for dx in range(1, NX) for k in range(len(near_offsets())) for dy in range(NY)]
+
+
+def near_slot(dx, k, dy):
+    return ((dx - 1) * len(near_offsets()) + k) * NY + dy
 
 
 def exchange_x(src, slots, send_sem, recv_sem):
@@ -169,12 +181,28 @@
     return finish
 
 
-def backward_scan(r1, t2, r2, plain_in, px, out, sems):
-    s1, q1, s2, q2, sf, qf, s3, q3, own_sem = sems
-    x, z, y = place()
-    await_bytes(r1.at[1:], q1.at[0])
+def backward_scan(r1, near, t2, r2, plain_in, px, out, sems):
+    s1, q1, sn, qn, s2, q2, sf, qf, s3, q3, own_sem = sems
+    x, z, y = place()
+    far = [(dz, dy) for dz in range(NZ) for dy in range(NY) if dz not in near_offsets()]
+    await_bytes(r1.at[0 : len(far)], q1.at[0])
+    total = jnp.zeros(r1.shape[1:], F32)
     plain = jnp.zeros(r1.shape[1:], F32)
+    for dz, dy in far:
+        one = r1[dz * NY + dy]
+        plain = plain + one
+        total = total + one * level_rows(bead_of(x, rem(z + (NZ - dz), NZ), rem(y + (NY - dy), NY)))
+    t2[0] = total
+    t2[1] = plain
+    exchange_x(t2.at[0], r2, s2, q2)
+
+    @pl.when(x != 0)
+    def _():
+        send(t2.at[1], plain_in.at[x], sf.at[0], qf.at[0], to_bead(bead_of(0, z, y)))
+
+    await_bytes(r1.at[0 : len(group_steps()) - len(far)], q1.at[1])
     total = jnp.zeros(r1.shape[1:], F32)
+    plain = jnp.zeros(r1.shape[1:], F32)
     for zs in range(NZ):
         kept = None
         for ys in range(NY):
@@ -183,13 +211,14 @@
             total = total + one * level_rows(bead_of(x, zs, ys))
             kept = total if kept is None else jnp.where(y == ys, total, kept)
         px[zs] = kept
-    t2[0] = total
-    t2[1] = plain
-    exchange_x(t2.at[0], r2, s2, q2)
-
-    @pl.when(x != 0)
-    def _():
-        send(t2.at[1], plain_in.at[x], sf.at[0], qf.at[0], to_bead(bead_of(0, z, y)))
+    await_bytes(near, qn.at[0])
+    base = jnp.zeros(r1.shape[1:], F32)
+    for dx, k, dy in near_slots():
+        xs = rem(x + (NX - dx), NX)
+        source = bead_of(xs, rem(z + (NZ - near_offsets()[k]), NZ), rem(y + (NY - dy), NY))
+        one = near[near_slot(dx, k, dy)]
+        plain = plain + one
+        base = base + jnp.where(xs < x, one * level_rows(source), 0.0)
 
     @pl.when(x == 0)
     def _():
@@ -197,7 +226,6 @@
         await_bytes(plain_in.at[1:], qf.at[0])
 
     await_bytes(r2.at[1:], q2.at[0])
-    base = jnp.zeros(r1.shape[1:], F32)
     for dx in range(1, NX):
         xs = rem(x + (NX - dx), NX)
         base = base + jnp.where(xs < x, r2[dx], 0.0)
@@ -223,6 +251,7 @@
     await_bytes(px.at[1:], q3.at[0])
     own.wait()
     await_bytes(r1.at[1:], s1.at[0])
+    await_bytes(near, sn.at[0])
     await_bytes(r2.at[1:], s2.at[0])
     await_bytes(px.at[1:], s3.at[0])
 
@@ -342,11 +371,12 @@
         force[zc, c, n : n + 1, :] = result[c : c + 1]
 
 
-def forces(neighbours, count, lefts, lefts_t, rights, places, even, odd, force, r1, send_sem, recv_sem):
+def forces(neighbours, count, lefts, lefts_t, rights, places, even, odd, force, r1, near, sems):
     x, z, y = place()
     tpc = rights.shape[0] // NZ
     half = NZ // 2
     bufs = (even, odd)
+    send_sem, recv_sem, near_send, near_recv = sems
 
     def offset(c):
         return half + lax.div(c, jnp.int32(2)) * (1 - rem(c, 2)) - lax.div(c + 1, jnp.int32(2)) * rem(c, 2)
@@ -361,11 +391,21 @@
             following = zc * tpc + n + 1 if n + 1 < tpc else after * tpc
             quotients(following, bufs[(n + 1) % 2], neighbours, lefts_t, rights)
             tile_force(zc * tpc + n, zc, n, bufs[n % 2], neighbours, lefts, places, force, count)
-        group_copy(force.at[zc], r1, send_sem, recv_sem, dz, 1).start()
+        first_near = NZ - len(near_offsets())
+        kind = jnp.minimum(jnp.maximum(c - first_near + 1, 0), 1)
+        group_copy(force.at[zc], r1, send_sem, recv_sem, dz, 1, kind).start()
 
         @pl.when(c < NZ - 1)
         def _():
-            group_copy(force.at[zc], r1, send_sem, recv_sem, dz, 0).start()
+            group_copy(force.at[zc], r1, send_sem, recv_sem, dz, 0, kind).start()
+
+        @pl.when(c >= first_near)
+        def _():
+            for dx in range(1, NX):
+                for dy in range(NY):
+                    device = to_bead(bead_of(rem(x + dx, NX), zc, rem(y + dy, NY)))
+                    slot = near_slot(dx, c - first_near, dy)
+                    send(force.at[zc], near.at[slot], near_send.at[0], near_recv.at[0], device)
 
         return carry
 
@@ -377,7 +417,7 @@
     counts, neighbours_in, border_in, section_in, out,
     neighbours, border, section, raw, land, halo, force,
     lefts, lefts_t, rights, places, even, odd,
-    r1f, t2f, r2f, first_in, pxf, r1b, t2b, r2b, plain_in, pxb,
+    r1f, t2f, r2f, first_in, pxf, r1b, t2b, r2b, plain_in, pxb, near,
     load_sem, *sems,
 ):
     x, z, y = place()
@@ -423,9 +463,9 @@
         for dz in tiles:
             prepare_halo(rem(z + (NZ - dz), NZ), halo, shifts, *refs)
     forces(
-        neighbours, count, lefts, lefts_t, rights, places, even, odd, force, r1b, sems[10], sems[11]
+        neighbours, count, lefts, lefts_t, rights, places, even, odd, force, r1b, near, sems[10:14]
     )
-    backward_scan(r1b, t2b, r2b, plain_in, pxb, out, sems[10:])
+    backward_scan(r1b, near, t2b, r2b, plain_in, pxb, out, sems[10:])
     finish()
 
 
@@ -492,9 +532,11 @@
             vmem(listed * TILE, TILE),
         ]
         + scan_buffers
+        + [vmem(len(near_slots()), *chunk)]
         + [DMA((3,))]
         + [one] * 6
         + [one, each] * 2
+        + [one, DMA((2,))]
         + [one] * 9,
         compiler_params=pltpu.CompilerParams(
             collective_id=0, has_side_effects=True, vmem_limit_bytes=24 * 2**20

time: 46.1 us -> 45.4 us (0.985); the launches traced: 45.9 us -> 44.7 us
  Pallas kernels: 43.8 us -> 42.5 us
    pallas_call x1, Pallas kernels: 43.8 us -> 42.5 us  [step(): pl.pallas_call(kernel, out_shape=jax.ShapeDtypeStruct(dense, F32), in_spe...]
where the time goes in v7:
time: 45.4 us; the launch traced here: 44.7 us
  Pallas kernels  42.5 us (94%)
  between operations  1.41 us (3%)
  other arithmetic  0.71 us (2%)
    pallas_call x1, Pallas kernels, step(): pl.pallas_call(kernel, out_shape=jax.ShapeDtypeStruct(dense, F32), in_spe...  42.5 us

profile of v7, /device:TPU:2, one launch (start us, length us, event | category | flops | bytes accessed | tf_op | source)
XLA Modules:
  0.0 44.7 jit_solution(77317761796703086)
XLA Ops:
  1.4 0.0 copy-start
  1.4 0.0 copy-start.1
  1.4 42.5 %path_step.1 = f32[3,8,4,128]{3,2,1,0:T(4,128)S(1)} custom-call(s32[1]{0:T(128)S(6)} %copy.11.counts, s32[8,32]{1,0:T(8,128)} %bitcast.13, s32[2,512]{1,0:T(2,128)} %bitcast.14, f32[3,8,4,128]{3,2,1,0:T(4,128)} %bitcast.8), custom_call_target="tpu_custom_call" | custom-call | tf_op jit(solution)/shard_map/path_step/pallas_call | solution.py:509
  43.9 0.0 copy-done
  43.9 0.0 copy-done.1
  43.9 0.7 %multiply_subtract_fusion = (f32[3,8,4,128]{3,2,1,0:T(4,128)}, f32[3,8,4,128]{3,2,1,0:T(4,128)}) fusion(f32[]{:T(128)S(6)} %mul_shard_map.7, f32[3,8,4,128]{3,2,1,0:T(4,128)S(1)} %bitcast.9, f32[]{:T(128)S(6)} %div.13, f32[3,8,4,128]{3,2,1,0:T(4,128)S(1)} %bitcast.10, f32[3,8,4,128]{3,2,1,0:T(4,128)S(1)} %path_step.1, f32[]{:T(128)S(6)} %max.3), kind=kLoop, calls=%fused_computation.2 | loop fusion | flops 233472 | bytes 245772 | tf_op jit(solution)/shard_map/sub | solution.py:486
Async XLA Ops:
  1.4 42.6 %copy-start = (f32[1,3,4096]{2,0,1:T(1,128)S(1)}, f32[1,3,4096]{2,0,1:T(1,128)}, u32[]{:S(2)}) copy-start(f32[1,3,4096]{2,0,1:T(1,128)} %param.5) | copy-start | bytes 147460
  1.4 42.6 %copy-start.1 = (f32[1,3,4096]{2,0,1:T(1,128)S(1)}, f32[1,3,4096]{2,0,1:T(1,128)}, u32[]{:S(2)}) copy-start(f32[1,3,4096]{2,0,1:T(1,128)} %param.6) | copy-start | bytes 147460

commit v8 on v7

--- a/solution.py
+++ b/solution.py
@@ -86,7 +86,7 @@
 
 
 def near_offsets():
-    return (1, NZ - 1, 0)
+    return (NZ - 2, 1, NZ - 1, 0) if NZ > 4 else (1, NZ - 1, 0)
 
 
 def near_slots():
@@ -121,7 +121,7 @@
     s1, q1, s2, q2, sf, qf, s3, q3, s4, q4 = sems
     x, z, y = place()
     slab, slabs = lax.axis_index("slab"), lax.axis_size("slab")
-    for dz, dy in reversed(group_steps()):
+    for dz, dy in sorted(group_steps(), key=lambda step: -reach(step[0]) - step[1]):
         group_copy(raw.at[rem(z + dz, NZ)], r1, s1, q1, dz, dy).start()
     r1[0] = raw[z]
     await_bytes(r1.at[1:], q1.at[0])
@@ -427,12 +427,12 @@
         pltpu.make_async_copy(border_in, border, load_sem.at[1]),
         pltpu.make_async_copy(neighbours_in, neighbours, load_sem.at[2]),
     ]
-    for load in loads:
-        load.start()
     barrier = pltpu.get_barrier_semaphore()
     greeted = partners()
     for device in greeted:
         pl.semaphore_signal(barrier, inc=1, device_id=device, device_id_type=MESH)
+    for load in loads:
+        load.start()
     for load in loads:
         load.wait()
     pack_chunks(section, border, raw)

time: 45.4 us -> 44.4 us (0.978)
  Pallas kernels: 42.5 us -> 41.7 us
    pallas_call x1, Pallas kernels: 42.5 us -> 41.7 us  [step(): pl.pallas_call(kernel, out_shape=jax.ShapeDtypeStruct(dense, F32), in_spe...]
where the time goes in v8:
time: 44.4 us; the launch traced here: 43.8 us
  Pallas kernels  41.7 us (94%)
  between operations  1.41 us (3%)
  other arithmetic  0.71 us (2%)
    pallas_call x1, Pallas kernels, step(): pl.pallas_call(kernel, out_shape=jax.ShapeDtypeStruct(dense, F32), in_spe...  41.7 us

profile of v8, /device:TPU:2, one launch (start us, length us, event | category | flops | bytes accessed | tf_op | source)
XLA Modules:
  0.0 43.8 jit_solution(14232484349144328358)
XLA Ops:
  1.4 0.0 copy-start
  1.4 0.0 copy-start.1
  1.4 41.7 %path_step.1 = f32[3,8,4,128]{3,2,1,0:T(4,128)S(1)} custom-call(s32[1]{0:T(128)S(6)} %copy.11.counts, s32[8,32]{1,0:T(8,128)} %bitcast.13, s32[2,512]{1,0:T(2,128)} %bitcast.14, f32[3,8,4,128]{3,2,1,0:T(4,128)} %bitcast.8), custom_call_target="tpu_custom_call" | custom-call | tf_op jit(solution)/shard_map/path_step/pallas_call | solution.py:509
  43.1 0.0 copy-done
  43.1 0.0 copy-done.1
  43.1 0.7 %multiply_subtract_fusion = (f32[3,8,4,128]{3,2,1,0:T(4,128)}, f32[3,8,4,128]{3,2,1,0:T(4,128)}) fusion(f32[]{:T(128)S(6)} %mul_shard_map.7, f32[3,8,4,128]{3,2,1,0:T(4,128)S(1)} %bitcast.9, f32[]{:T(128)S(6)} %div.13, f32[3,8,4,128]{3,2,1,0:T(4,128)S(1)} %bitcast.10, f32[3,8,4,128]{3,2,1,0:T(4,128)S(1)} %path_step.1, f32[]{:T(128)S(6)} %max.3), kind=kLoop, calls=%fused_computation.2 | loop fusion | flops 233472 | bytes 245772 | tf_op jit(solution)/shard_map/sub | solution.py:486
Async XLA Ops:
  1.4 41.7 %copy-start = (f32[1,3,4096]{2,0,1:T(1,128)S(1)}, f32[1,3,4096]{2,0,1:T(1,128)}, u32[]{:S(2)}) copy-start(f32[1,3,4096]{2,0,1:T(1,128)} %param.5) | copy-start | bytes 147460
  1.4 41.7 %copy-start.1 = (f32[1,3,4096]{2,0,1:T(1,128)S(1)}, f32[1,3,4096]{2,0,1:T(1,128)}, u32[]{:S(2)}) copy-start(f32[1,3,4096]{2,0,1:T(1,128)} %param.6) | copy-start | bytes 147460

commit v9 on v8

--- a/solution.py
+++ b/solution.py
@@ -358,8 +358,8 @@
         q = buf[k * TILE : (k + 2) * TILE, :]
         r = 1.0 / q
         r2 = r * r
-        d = jnp.maximum(r2 - r, 0.0)
-        f = ((d * d) * (r2 * r - 0.5 * reach_sq**3)).astype(BF16)
+        d = jnp.maximum((r2 - r).astype(BF16), jnp.zeros(q.shape, BF16))
+        f = (d * d) * (r2 * r - 0.5 * reach_sq**3).astype(BF16)
         x = jnp.concatenate([lefts[neighbours[k, i]], lefts[neighbours[k + 1, i]]], axis=1)
         total = total + jnp.dot(x, f, preferred_element_type=F32)
     moved = total[0:8] + total[8:16] + total[16:24]
@@ -383,24 +383,40 @@
 
     quotients(rem(z + half, NZ) * tpc, even, neighbours, lefts_t, rights)
 
-    def chunk(c, carry):
-        dz = offset(c)
-        zc = rem(z + dz, NZ)
+    first_near = NZ - len(near_offsets())
+
+    def compute(c):
+        zc = rem(z + offset(c), NZ)
         after = rem(z + offset(jnp.minimum(c + 1, NZ - 1)), NZ)
         for n in range(tpc):
             following = zc * tpc + n + 1 if n + 1 < tpc else after * tpc
             quotients(following, bufs[(n + 1) % 2], neighbours, lefts_t, rights)
             tile_force(zc * tpc + n, zc, n, bufs[n % 2], neighbours, lefts, places, force, count)
-        first_near = NZ - len(near_offsets())
+
+    def leave(c, kind, dy):
+        dz = offset(c)
+        group_copy(force.at[rem(z + dz, NZ)], r1, send_sem, recv_sem, dz, dy, kind).start()
+
+    def pair(g, carry):
+        for m in range(2):
+            compute(2 * g + m)
+        for m in range(2):
+            for dy in range(NY):
+                leave(2 * g + m, 0, dy)
+        return carry
+
+    def chunk(c, carry):
+        compute(c)
         kind = jnp.minimum(jnp.maximum(c - first_near + 1, 0), 1)
-        group_copy(force.at[zc], r1, send_sem, recv_sem, dz, 1, kind).start()
+        leave(c, kind, 1)
 
         @pl.when(c < NZ - 1)
         def _():
-            group_copy(force.at[zc], r1, send_sem, recv_sem, dz, 0, kind).start()
+            leave(c, kind, 0)
 
         @pl.when(c >= first_near)
         def _():
+            zc = rem(z + offset(c), NZ)
             for dx in range(1, NX):
                 for dy in range(NY):
                     device = to_bead(bead_of(rem(x + dx, NX), zc, rem(y + dy, NY)))
@@ -409,7 +425,9 @@
 
         return carry
 
-    lax.fori_loop(0, NZ, chunk, 0)
+    pairs = (first_near - 1) // 2
+    lax.fori_loop(0, pairs, pair, 0)
+    lax.fori_loop(2 * pairs, NZ, chunk, 0)
     r1[0] = force[z]
 
 

time: 44.4 us -> 43.5 us (0.980)
  Pallas kernels: 41.7 us -> 41 us
    pallas_call x1, Pallas kernels: 41.7 us -> 41 us  [step(): pl.pallas_call(kernel, out_shape=jax.ShapeDtypeStruct(dense, F32), in_spe...]
where the time goes in v9:
time: 43.5 us; the launch traced here: 43.2 us
  Pallas kernels  41 us (94%)
  between operations  1.41 us (3%)
  other arithmetic  0.71 us (2%)
    pallas_call x1, Pallas kernels, step(): pl.pallas_call(kernel, out_shape=jax.ShapeDtypeStruct(dense, F32), in_spe...  41 us

profile of v9, /device:TPU:2, one launch (start us, length us, event | category | flops | bytes accessed | tf_op | source)
XLA Modules:
  0.0 43.2 jit_solution(1597567357189894590)
XLA Ops:
  1.4 0.0 copy-start
  1.4 0.0 copy-start.1
  1.4 41.0 %path_step.1 = f32[3,8,4,128]{3,2,1,0:T(4,128)S(1)} custom-call(s32[1]{0:T(128)S(6)} %copy.11.counts, s32[8,32]{1,0:T(8,128)} %bitcast.13, s32[2,512]{1,0:T(2,128)} %bitcast.14, f32[3,8,4,128]{3,2,1,0:T(4,128)} %bitcast.8), custom_call_target="tpu_custom_call" | custom-call | tf_op jit(solution)/shard_map/path_step/pallas_call | solution.py:527
  42.4 0.0 copy-done
  42.4 0.0 copy-done.1
  42.4 0.7 %multiply_subtract_fusion = (f32[3,8,4,128]{3,2,1,0:T(4,128)}, f32[3,8,4,128]{3,2,1,0:T(4,128)}) fusion(f32[]{:T(128)S(6)} %mul_shard_map.7, f32[3,8,4,128]{3,2,1,0:T(4,128)S(1)} %bitcast.9, f32[]{:T(128)S(6)} %div.13, f32[3,8,4,128]{3,2,1,0:T(4,128)S(1)} %bitcast.10, f32[3,8,4,128]{3,2,1,0:T(4,128)S(1)} %path_step.1, f32[]{:T(128)S(6)} %max.3), kind=kLoop, calls=%fused_computation.2 | loop fusion | flops 233472 | bytes 245772 | tf_op jit(solution)/shard_map/sub | solution.py:504
Async XLA Ops:
  1.4 41.1 %copy-start = (f32[1,3,4096]{2,0,1:T(1,128)S(1)}, f32[1,3,4096]{2,0,1:T(1,128)}, u32[]{:S(2)}) copy-start(f32[1,3,4096]{2,0,1:T(1,128)} %param.5) | copy-start | bytes 147460
  1.4 41.1 %copy-start.1 = (f32[1,3,4096]{2,0,1:T(1,128)S(1)}, f32[1,3,4096]{2,0,1:T(1,128)}, u32[]{:S(2)}) copy-start(f32[1,3,4096]{2,0,1:T(1,128)} %param.6) | copy-start | bytes 147460

commit v10 on v9

--- a/solution.py
+++ b/solution.py
@@ -200,9 +200,24 @@
     def _():
         send(t2.at[1], plain_in.at[x], sf.at[0], qf.at[0], to_bead(bead_of(0, z, y)))
 
+    def gather_near(k, base, plain):
+        await_bytes(near.at[0 : (NX - 1) * NY], qn.at[k])
+        for dx in range(1, NX):
+            for dy in range(NY):
+                xs = rem(x + (NX - dx), NX)
+                source = bead_of(xs, rem(z + (NZ - near_offsets()[k]), NZ), rem(y + (NY - dy), NY))
+                one = near[near_slot(dx, k, dy)]
+                plain = plain + one
+                base = base + jnp.where(xs < x, one * level_rows(source), 0.0)
+        return base, plain
+
+    base = jnp.zeros(r1.shape[1:], F32)
+    plain = jnp.zeros(r1.shape[1:], F32)
+    last = len(near_offsets()) - 1
+    for k in range(last):
+        base, plain = gather_near(k, base, plain)
     await_bytes(r1.at[0 : len(group_steps()) - len(far)], q1.at[1])
     total = jnp.zeros(r1.shape[1:], F32)
-    plain = jnp.zeros(r1.shape[1:], F32)
     for zs in range(NZ):
         kept = None
         for ys in range(NY):
@@ -211,14 +226,7 @@
             total = total + one * level_rows(bead_of(x, zs, ys))
             kept = total if kept is None else jnp.where(y == ys, total, kept)
         px[zs] = kept
-    await_bytes(near, qn.at[0])
-    base = jnp.zeros(r1.shape[1:], F32)
-    for dx, k, dy in near_slots():
-        xs = rem(x + (NX - dx), NX)
-        source = bead_of(xs, rem(z + (NZ - near_offsets()[k]), NZ), rem(y + (NY - dy), NY))
-        one = near[near_slot(dx, k, dy)]
-        plain = plain + one
-        base = base + jnp.where(xs < x, one * level_rows(source), 0.0)
+    base, plain = gather_near(last, base, plain)
 
     @pl.when(x == 0)
     def _():
@@ -407,21 +415,21 @@
 
     def chunk(c, carry):
         compute(c)
+        @pl.when(c >= first_near)
+        def _():
+            zc = rem(z + offset(c), NZ)
+            for dx in sorted(range(1, NX), key=lambda step: -min(step, NX - step)):
+                for dy in reversed(range(NY)):
+                    device = to_bead(bead_of(rem(x + dx, NX), zc, rem(y + dy, NY)))
+                    slot = near_slot(dx, c - first_near, dy)
+                    send(force.at[zc], near.at[slot], near_send.at[0], near_recv.at[c - first_near], device)
+
         kind = jnp.minimum(jnp.maximum(c - first_near + 1, 0), 1)
         leave(c, kind, 1)
 
         @pl.when(c < NZ - 1)
         def _():
             leave(c, kind, 0)
-
-        @pl.when(c >= first_near)
-        def _():
-            zc = rem(z + offset(c), NZ)
-            for dx in range(1, NX):
-                for dy in range(NY):
-                    device = to_bead(bead_of(rem(x + dx, NX), zc, rem(y + dy, NY)))
-                    slot = near_slot(dx, c - first_near, dy)
-                    send(force.at[zc], near.at[slot], near_send.at[0], near_recv.at[0], device)
 
         return carry
 
@@ -554,8 +562,8 @@
         + [DMA((3,))]
         + [one] * 6
         + [one, each] * 2
-        + [one, DMA((2,))]
-        + [one] * 9,
+        + [one, DMA((2,)), one, DMA((len(near_offsets()),))]
+        + [one] * 7,
         compiler_params=pltpu.CompilerParams(
             collective_id=0, has_side_effects=True, vmem_limit_bytes=24 * 2**20
         ),

time: 43.5 us -> 43.1 us (level)
  no operation moved by 1% of the time
where the time goes in v10:
time: 43.1 us; the launch traced here: 43 us
  Pallas kernels  40.9 us (95%)
  between operations  1.41 us (3%)
  other arithmetic  0.71 us (2%)
    pallas_call x1, Pallas kernels, step(): pl.pallas_call(kernel, out_shape=jax.ShapeDtypeStruct(dense, F32), in_spe...  40.9 us

profile of v10, /device:TPU:2, one launch (start us, length us, event | category | flops | bytes accessed | tf_op | source)
XLA Modules:
  0.0 43.0 jit_solution(5345136153703743320)
XLA Ops:
  1.4 0.0 copy-start
  1.4 0.0 copy-start.1
  1.4 40.9 %path_step.1 = f32[3,8,4,128]{3,2,1,0:T(4,128)S(1)} custom-call(s32[1]{0:T(128)S(6)} %copy.11.counts, s32[8,32]{1,0:T(8,128)} %bitcast.13, s32[2,512]{1,0:T(2,128)} %bitcast.14, f32[3,8,4,128]{3,2,1,0:T(4,128)} %bitcast.8), custom_call_target="tpu_custom_call" | custom-call | tf_op jit(solution)/shard_map/path_step/pallas_call | solution.py:535
  42.3 0.0 copy-done
  42.3 0.0 copy-done.1
  42.3 0.7 %multiply_subtract_fusion = (f32[3,8,4,128]{3,2,1,0:T(4,128)}, f32[3,8,4,128]{3,2,1,0:T(4,128)}) fusion(f32[]{:T(128)S(6)} %mul_shard_map.7, f32[3,8,4,128]{3,2,1,0:T(4,128)S(1)} %bitcast.9, f32[]{:T(128)S(6)} %div.13, f32[3,8,4,128]{3,2,1,0:T(4,128)S(1)} %bitcast.10, f32[3,8,4,128]{3,2,1,0:T(4,128)S(1)} %path_step.1, f32[]{:T(128)S(6)} %max.3), kind=kLoop, calls=%fused_computation.2 | loop fusion | flops 233472 | bytes 245772 | tf_op jit(solution)/shard_map/sub | solution.py:512
Async XLA Ops:
  1.4 40.9 %copy-start = (f32[1,3,4096]{2,0,1:T(1,128)S(1)}, f32[1,3,4096]{2,0,1:T(1,128)}, u32[]{:S(2)}) copy-start(f32[1,3,4096]{2,0,1:T(1,128)} %param.5) | copy-start | bytes 147460
  1.4 40.9 %copy-start.1 = (f32[1,3,4096]{2,0,1:T(1,128)S(1)}, f32[1,3,4096]{2,0,1:T(1,128)}, u32[]{:S(2)}) copy-start(f32[1,3,4096]{2,0,1:T(1,128)} %param.6) | copy-start | bytes 147460

commit v11 on v10

--- a/solution.py
+++ b/solution.py
@@ -121,10 +121,19 @@
     s1, q1, s2, q2, sf, qf, s3, q3, s4, q4 = sems
     x, z, y = place()
     slab, slabs = lax.axis_index("slab"), lax.axis_size("slab")
-    for dz, dy in sorted(group_steps(), key=lambda step: -reach(step[0]) - step[1]):
-        group_copy(raw.at[rem(z + dz, NZ)], r1, s1, q1, dz, dy).start()
+    steps = sorted(group_steps(), key=lambda step: -reach(step[0]) - step[1])
+    for dz, dy in steps:
+        group_copy(raw.at[rem(z + dz, NZ)], r1, s1, q1, dz, dy, reach(dz)).start()
     r1[0] = raw[z]
-    await_bytes(r1.at[1:], q1.at[0])
+    total = jnp.where(bead_of(x, z, y) == 0, 0.0, raw[z])
+    for distance in range(NZ // 2 + 1):
+        group = [step for step in steps if reach(step[0]) == distance]
+        await_bytes(r1.at[0 : len(group)], q1.at[distance])
+        for dz, dy in group:
+            source = bead_of(x, rem(z + (NZ - dz), NZ), rem(y + (NY - dy), NY))
+            total = total + jnp.where(source == 0, 0.0, r1[dz * NY + dy])
+    t2[0] = total
+    exchange_x(t2.at[0], r2, s2, q2)
 
     @pl.when(x == 0)
     def _():
@@ -143,8 +152,6 @@
             total = total + one
             kept = total if kept is None else jnp.where(y == ys, total, kept)
         px[zs] = kept
-    t2[0] = total
-    exchange_x(t2.at[0], r2, s2, q2)
 
     @pl.when(x != 0)
     def _():
@@ -560,7 +567,8 @@
         + scan_buffers
         + [vmem(len(near_slots()), *chunk)]
         + [DMA((3,))]
-        + [one] * 6
+        + [one, DMA((NZ // 2 + 1,))]
+        + [one] * 4
         + [one, each] * 2
         + [one, DMA((2,)), one, DMA((len(near_offsets()),))]
         + [one] * 7,

time: 43.1 us -> 43.1 us (level)
  no operation moved by 1% of the time
where the time goes in v11:
time: 43.1 us; the launch traced here: 43 us
  Pallas kernels  40.9 us (95%)
  between operations  1.41 us (3%)
  other arithmetic  0.71 us (2%)
    pallas_call x1, Pallas kernels, step(): pl.pallas_call(kernel, out_shape=jax.ShapeDtypeStruct(dense, F32), in_spe...  40.9 us

profile of v11, /device:TPU:2, one launch (start us, length us, event | category | flops | bytes accessed | tf_op | source)
XLA Modules:
  0.0 43.0 jit_solution(16931875327348898369)
XLA Ops:
  1.4 0.0 copy-start
  1.4 0.0 copy-start.1
  1.4 40.9 %path_step.1 = f32[3,8,4,128]{3,2,1,0:T(4,128)S(1)} custom-call(s32[1]{0:T(128)S(6)} %copy.11.counts, s32[8,32]{1,0:T(8,128)} %bitcast.13, s32[2,512]{1,0:T(2,128)} %bitcast.14, f32[3,8,4,128]{3,2,1,0:T(4,128)} %bitcast.8), custom_call_target="tpu_custom_call" | custom-call | tf_op jit(solution)/shard_map/path_step/pallas_call | solution.py:542
  42.3 0.0 copy-done
  42.3 0.0 copy-done.1
  42.3 0.7 %multiply_subtract_fusion = (f32[3,8,4,128]{3,2,1,0:T(4,128)}, f32[3,8,4,128]{3,2,1,0:T(4,128)}) fusion(f32[]{:T(128)S(6)} %mul_shard_map.7, f32[3,8,4,128]{3,2,1,0:T(4,128)S(1)} %bitcast.9, f32[]{:T(128)S(6)} %div.13, f32[3,8,4,128]{3,2,1,0:T(4,128)S(1)} %bitcast.10, f32[3,8,4,128]{3,2,1,0:T(4,128)S(1)} %path_step.1, f32[]{:T(128)S(6)} %max.3), kind=kLoop, calls=%fused_computation.2 | loop fusion | flops 233472 | bytes 245772 | tf_op jit(solution)/shard_map/sub | solution.py:519
Async XLA Ops:
  1.4 40.9 %copy-start = (f32[1,3,4096]{2,0,1:T(1,128)S(1)}, f32[1,3,4096]{2,0,1:T(1,128)}, u32[]{:S(2)}) copy-start(f32[1,3,4096]{2,0,1:T(1,128)} %param.5) | copy-start | bytes 147460
  1.4 40.9 %copy-start.1 = (f32[1,3,4096]{2,0,1:T(1,128)S(1)}, f32[1,3,4096]{2,0,1:T(1,128)}, u32[]{:S(2)}) copy-start(f32[1,3,4096]{2,0,1:T(1,128)} %param.6) | copy-start | bytes 147460

commit v12 on v10

--- a/solution.py
+++ b/solution.py
@@ -237,9 +237,6 @@
     for dx in range(1, NX):
         xs = rem(x + (NX - dx), NX)
         base = base + jnp.where(xs < x, r2[dx], 0.0)
-    for zs in range(NZ):
-        px[zs] = px[zs] + base
-
     @pl.when((x == 0) & (y == 0))
     def _():
         everything = plain_in[0]
@@ -249,6 +246,7 @@
 
     for dz in near_first()[::-1] + [0]:
         tz = rem(z + dz, NZ)
+        px[tz] = px[tz] + jnp.where(bead_of(x, tz, y) == 0, 0.0, base)
         if dz:
             device = to_bead(bead_of(x, tz, y))
             send(px.at[tz], out.at[:, z], s3.at[0], q3.at[0], device)

time: 43.1 us -> 43.1 us (level)
  no operation moved by 1% of the time
where the time goes in v12:
time: 43.1 us; the launch traced here: 43 us
  Pallas kernels  40.8 us (95%)
  between operations  1.41 us (3%)
  other arithmetic  0.71 us (2%)
    pallas_call x1, Pallas kernels, step(): pl.pallas_call(kernel, out_shape=jax.ShapeDtypeStruct(dense, F32), in_spe...  40.8 us

profile of v12, /device:TPU:2, one launch (start us, length us, event | category | flops | bytes accessed | tf_op | source)
XLA Modules:
  0.0 43.0 jit_solution(11740256041692705353)
XLA Ops:
  1.4 0.0 copy-start
  1.4 0.0 copy-start.1
  1.4 40.8 %path_step.1 = f32[3,8,4,128]{3,2,1,0:T(4,128)S(1)} custom-call(s32[1]{0:T(128)S(6)} %copy.11.counts, s32[8,32]{1,0:T(8,128)} %bitcast.13, s32[2,512]{1,0:T(2,128)} %bitcast.14, f32[3,8,4,128]{3,2,1,0:T(4,128)} %bitcast.8), custom_call_target="tpu_custom_call" | custom-call | tf_op jit(solution)/shard_map/path_step/pallas_call | solution.py:533
  42.2 0.0 copy-done
  42.2 0.0 copy-done.1
  42.3 0.7 %multiply_subtract_fusion = (f32[3,8,4,128]{3,2,1,0:T(4,128)}, f32[3,8,4,128]{3,2,1,0:T(4,128)}) fusion(f32[]{:T(128)S(6)} %mul_shard_map.7, f32[3,8,4,128]{3,2,1,0:T(4,128)S(1)} %bitcast.9, f32[]{:T(128)S(6)} %div.13, f32[3,8,4,128]{3,2,1,0:T(4,128)S(1)} %bitcast.10, f32[3,8,4,128]{3,2,1,0:T(4,128)S(1)} %path_step.1, f32[]{:T(128)S(6)} %max.3), kind=kLoop, calls=%fused_computation.2 | loop fusion | flops 233472 | bytes 245772 | tf_op jit(solution)/shard_map/sub | solution.py:510
Async XLA Ops:
  1.4 40.9 %copy-start = (f32[1,3,4096]{2,0,1:T(1,128)S(1)}, f32[1,3,4096]{2,0,1:T(1,128)}, u32[]{:S(2)}) copy-start(f32[1,3,4096]{2,0,1:T(1,128)} %param.5) | copy-start | bytes 147460
  1.4 40.9 %copy-start.1 = (f32[1,3,4096]{2,0,1:T(1,128)S(1)}, f32[1,3,4096]{2,0,1:T(1,128)}, u32[]{:S(2)}) copy-start(f32[1,3,4096]{2,0,1:T(1,128)} %param.6) | copy-start | bytes 147460
